TPU v7x, 512 devices: a whole 4x8x8 slice. The times are simulated.
512 devices in a mesh: section: 16 (over x, z_hi), rep: 32 (over z_lo, y, core).
Axes of the slice: x: 4, y: 8, z: 8 (z_hi: 4, z_lo: 2; z = z_hi * 2 + z_lo), core: 2. Of those that a mesh axis runs over, the one named last changes fastest.
Arguments:
- features: bfloat16 [131072, 128], P(('section', 'rep')), may hold values from -6 to 6
- inv_degree: float32 [131072], P(('section', 'rep')), may hold values from 0.03 to 0.3
- weight: bfloat16 [128, 128], replicated, may hold values from -0.5 to 0.5
- bias_vector: float32 [128], replicated, may hold values from -3 to 3
- tile_values: bfloat16 [512, 16, 8, 128, 128], P(('section', 'rep')), may hold values from 0 to 1
- tile_rows: int32 [512, 16, 8], P(('section', 'rep')), may hold values from 0 to 63, as said below
- tile_cols: int32 [512, 16, 8], P(('section', 'rep')), may hold values from 0 to 1
- tile_counts: int32 [512, 16], P(('section', 'rep')), may hold values from 0 to 8, as said below
Outputs:
- output: bfloat16 [131072, 128], P(('section', 'rep'))
Inputs may be any that keep to these rules, and one draw needn't show every extreme that they name: `tile_rows`: within one device and column section no pair of tile row and tile column repeats among the slots. `tile_counts`: slots beyond the count are not read. In every draw some device has 8 live slots for some column section.
All inputs are finite; a program needn't handle non-finite values.
Results may differ from a plain program's by a relative error of at most 0.023.
Values may be sent and summed in bfloat16 or wider, within the bound.
A program may use at most 64 MiB of HBM per device.

v0:
```python
import jax
import jax.numpy as jnp
from jax import lax
from jax.sharding import PartitionSpec as P


def section_terms(partial_value, pieces, values, slot_rows, slot_cols, slot_counts):
    groups, slot_count = slot_rows.shape
    slot_ids = lax.broadcasted_iota(jnp.int32, (groups, slot_count), 1)
    section_ids = lax.broadcasted_iota(jnp.int32, (groups, slot_count), 0)
    alive_mask = slot_ids < slot_counts[:, None]
    sources = pieces[section_ids, slot_cols]
    products = jnp.einsum("tkij,tkjf->tkif", values, sources, preferred_element_type=jnp.float32)
    products = jnp.where(alive_mask[:, :, None, None], products, 0.0)
    return partial_value.at[slot_rows.reshape(-1)].add(
        products.reshape(groups * slot_count, products.shape[2], products.shape[3])
    )


def shards(
    features, inv_degree, weight, bias_vector, tile_values, tile_rows, tile_cols, tile_counts
):
    section_count = lax.axis_size("section")
    rep_count = lax.axis_size("rep")
    rows_dev, feat_width = features.shape
    tile_size = tile_values.shape[-1]
    rows_per = rows_dev // tile_size
    scaled = (inv_degree[:, None] * features.astype(jnp.float32)).astype(jnp.bfloat16)
    values = tile_values[0]
    slot_rows = tile_rows[0]
    slot_cols = tile_cols[0]
    slot_counts = tile_counts[0]
    partial_value = jnp.zeros((rep_count * rows_per, tile_size, feat_width), jnp.float32)
    gathered = lax.all_gather(scaled, "section", axis=0, tiled=True)
    pieces = gathered.reshape(section_count, rows_per, tile_size, feat_width)
    partial_value = section_terms(partial_value, pieces, values, slot_rows, slot_cols, slot_counts)
    flat_partial = partial_value.reshape(rep_count * rows_dev, feat_width)
    summed = lax.psum_scatter(
        flat_partial.astype(jnp.bfloat16), "rep", scatter_dimension=0, tiled=True
    ).astype(jnp.float32)
    normed = (inv_degree[:, None] * summed).astype(jnp.bfloat16)
    hidden = jnp.dot(normed, weight, preferred_element_type=jnp.float32) + bias_vector
    return jnp.maximum(hidden, 0.0).astype(jnp.bfloat16)


def solution(mesh):
    return jax.shard_map(
        shards,
        mesh=mesh,
        in_specs=(
            P(("section", "rep"), None),
            P(("section", "rep")),
            P(),
            P(),
            P(("section", "rep"), None, None, None, None),
            P(("section", "rep"), None, None),
            P(("section", "rep"), None, None),
            P(("section", "rep"), None),
        ),
        out_specs=P(("section", "rep"), None),
        check_vma=False,
    )
```

profile of v0, /device:TPU:6, one launch (start us, length us, event | category | flops | bytes accessed | tf_op | source)
XLA Modules:
  0.0 258.5 jit_solution(8098084154914727275)
XLA Ops:
  6.5 0.0 copy-start
  6.5 0.0 all-gather.2.cloned.1.call-start
  6.5 1.6 multiply_convert_fusion.1
  8.1 0.0 all-gather.2.cloned.1.call-update
  8.1 0.0 reduce-scatter.2.cloned.1.call-start
  8.2 0.7 fusion.9
  8.9 0.1 copy.13
  9.0 0.1 reshape.102
  9.1 0.8 copy.12
  9.8 0.1 reshape_squeeze.3
  9.9 0.7 iota_compare_fusion
  10.7 62.4 %all-gather.2.cloned.1.call-done = bf16[4096,128]{1,0:T(8,128)(2,1)} async-done(((bf16[256,128]{1,0:T(8,128)(2,1)}), bf16[4096,128]{1,0:T(8,128)(2,1)}) %all-gather.2.cloned.1.call-update) | async-done | bytes 1048592 | tf_op jit(solution)/shard_map/all_gather | solution.py:34
  73.1 4.3 %gather_fusion = bf16[128,128,128]{2,1,0:T(8,128)(2,1)} fusion(bf16[16,2,128,128]{3,2,1,0:T(8,128)(2,1)} %bitcast.23, s32[128]{0:T(128)S(1)} %reshape.102), kind=kCustom, calls=%fused_computation | custom fusion | bytes 8389632 | tf_op jit(solution)/shard_map/gather | solution.py:12
  77.3 9.8 %broadcast_select_fusion = f32[16,8,128,128]{3,2,1,0:T(8,128)} fusion(pred[16,8]{1,0:T(8,128)(4,1)S(1)} %iota_compare_fusion, bf16[16,8,128,128]{3,2,1,0:T(8,128)(2,1)} %bitcast.22, bf16[1,16,8,128,128]{4,3,2,1,0:T(8,128)(2,1)} %param.12), kind=kOutput, calls=%fused_computation.4 | convolution fusion | flops 538968064 | bytes 16777344 | tf_op jit(solution)/shard_map/tkij,tkjf->tkif/dot_general | solution.py:13
  87.2 9.0 %copy.15 = f32[128,128,128]{2,1,0:T(8,128)} copy(f32[128,128,128]{1,2,0:T(8,128)} %bitcast.21) | data formatting | bytes 16777216 | tf_op jit(solution)/shard_map/reshape | solution.py:16
  96.2 2.5 broadcast_in_dim.14
  98.6 26.6 %scatter_fusion = f32[64,128,128]{2,1,0:T(8,128)} fusion(f32[64,128,128]{2,1,0:T(8,128)} %broadcast_in_dim.14, s32[128]{0:T(128)S(1)} %fusion.10, f32[128,128,128]{2,1,0:T(8,128)} %copy.15), kind=kCustom, calls=%fused_computation.1 | custom fusion | flops 2097152 | bytes 25166336 | tf_op jit(solution)/shard_map/scatter-add | solution.py:15
  125.2 0.0 copy-start.1
  125.2 0.0 copy-start.2
  125.2 3.9 %convert_element_type.23 = bf16[64,128,128]{2,1,0:T(8,128)(2,1)} convert(f32[64,128,128]{2,1,0:T(8,128)} %scatter_fusion) | non-fusion elementwise | flops 1048576 | bytes 6291456 | tf_op jit(solution)/shard_map/convert_element_type | solution.py:39
  129.2 0.0 reduce-scatter.2.cloned.1.call-update
  129.2 120.8 %reduce-scatter.2.cloned.1.call-done = bf16[256,128]{1,0:T(8,128)(2,1)} async-done(((bf16[8192,128]{1,0:T(8,128)(2,1)}), bf16[256,128]{1,0:T(8,128)(2,1)}) %reduce-scatter.2.cloned.1.call-update) | async-done | bytes 65552 | tf_op jit(solution)/shard_map/reduce_scatter | solution.py:38
  250.0 0.0 copy-done
  250.0 0.0 copy-done.1
  250.0 0.0 copy-done.2
  250.0 1.7 fusion.5
  (1 shorter events, 0.0 us)
Async XLA Ops:
  6.5 243.5 %copy-start = (bf16[128,128]{1,0:T(8,128)(2,1)S(1)}, bf16[128,128]{1,0:T(8,128)(2,1)}, u32[]{:S(2)}) copy-start(bf16[128,128]{1,0:T(8,128)(2,1)} %param.10) | copy-start | bytes 98308
  6.5 66.5 %all-gather.2.cloned.1.call-start = ((), (), s32[]{:S(2)}) async-start(), calls=%async_computation.1 | async-start | bytes 1114112 | tf_op jit(solution)/shard_map/all_gather | solution.py:34
  8.1 241.9 %reduce-scatter.2.cloned.1.call-start = ((), (), s32[]{:S(2)}) async-start(), calls=%async_computation.2 | async-start | bytes 2162688 | tf_op jit(solution)/shard_map/reduce_scatter | solution.py:38
  125.2 124.8 %copy-start.1 = (f32[256]{0:T(256)S(1)}, f32[256]{0:T(256)}, u32[]{:S(2)}) copy-start(f32[256]{0:T(256)} %param.9) | copy-start | bytes 3076
  125.2 124.8 %copy-start.2 = (f32[128]{0:T(128)S(1)}, f32[128]{0:T(128)}, u32[]{:S(2)}) copy-start(f32[128]{0:T(128)} %param.11) | copy-start | bytes 1540
Sparse Core Ops, SparseCore 0:
  10.3 62.6 all-gather.1
  129.3 120.6 reduce-scatter.1
where the time goes:
time: 259 us
  waiting for transfers between devices  183 us (71%)
  other arithmetic  33.5 us (13%)
  local copies, waits for them, and re-layouts  16.8 us (6%)
  between operations  13.4 us (5%)
  matrix products  11.5 us (4%)
    reduce_scatter x1, waiting for transfers between devices, shards(): lax.psum_scatter(flat_partial.astype(jnp.bfloat16), 'rep', scatter_dimens...  121 us
    all_gather x1, waiting for transfers between devices, shards(): gathered = lax.all_gather(scaled, 'section', axis=0, tiled=True)  62.4 us
    scatter-add x1, other arithmetic, section_terms(): partial_value.at[slot_rows.reshape(-1)]  26.6 us
    dot_general x1, matrix products, section_terms(): jnp.einsum('tkij,tkjf->tkif', values, sources, preferred_element_type=jnp...  9.82 us
    reshape x1, local copies, waits for them, and re-layouts, section_terms(): products.reshape(groups * slot_count, products.shape[2], products.shape[3])  9 us
  transfers between devices with their start and end apart: 2, of which 2 were waited for; matrix products, arithmetic and copies ran while one was open for 1% of the time, Pallas kernels for 0%

commit v1 on v0

v1 whole, which is shorter than its diff:
```python
import jax
import jax.numpy as jnp
from jax import lax
from jax.experimental import pallas as pl
from jax.experimental.pallas import tpu as pltpu
from jax.sharding import PartitionSpec as P

MESH = pl.DeviceIdType.MESH
VMEM_LIMIT = 60 * 1024 * 1024


def meet(axis, peers):
    barrier = pltpu.get_barrier_semaphore()
    for peer in peers:
        pl.semaphore_signal(barrier, inc=1, device_id={axis: peer}, device_id_type=MESH)
    pl.semaphore_wait(barrier, len(peers))


def gather_kernel(own_ref, out_ref, send_sems, recv_sems, local_sem):
    me = lax.axis_index("section")
    x, z = me // 4, me % 4
    half = own_ref.shape[0] // 2

    def sec(dx, dz):
        return ((x + dx) % 4) * 4 + (z + dz) % 4

    zp, zm, xp, xm = sec(0, 1), sec(0, 3), sec(1, 0), sec(3, 0)
    meet("section", (zp, zm, xp, xm))
    sends = []

    def send(slot, h, peer, own=False):
        rows = pl.ds(h * half, half)
        copy = pltpu.make_async_remote_copy(
            src_ref=own_ref.at[rows] if own else out_ref.at[slot, rows],
            dst_ref=out_ref.at[slot, rows],
            send_sem=send_sems.at[len(sends)],
            recv_sem=recv_sems.at[slot, h],
            device_id={"section": peer},
            device_id_type=MESH,
        )
        copy.start()
        sends.append(copy)

    waited = set()

    def need(dx, dz, h):
        if (dx, dz, h) in waited:
            return
        waited.add((dx, dz, h))
        slot, rows = sec(dx, dz), pl.ds(h * half, half)
        pltpu.make_async_remote_copy(
            src_ref=out_ref.at[slot, rows],
            dst_ref=out_ref.at[slot, rows],
            send_sem=send_sems.at[0],
            recv_sem=recv_sems.at[slot, h],
            device_id={"section": zp},
            device_id_type=MESH,
        ).wait_recv()

    for h, peer in ((0, zp), (1, zm), (1, zp), (0, zm), (0, xp), (1, xm), (1, xp), (0, xm)):
        send(me, h, peer, own=True)
    keep = pltpu.make_async_copy(own_ref, out_ref.at[me], local_sem)
    keep.start()

    need(0, 3, 0)
    send(sec(0, 3), 0, zp)
    need(0, 1, 1)
    send(sec(0, 1), 1, zm)
    send(sec(0, 3), 0, xp)
    send(sec(0, 1), 1, xm)
    need(3, 0, 0)
    send(sec(3, 0), 0, xp)
    need(1, 0, 1)
    send(sec(1, 0), 1, xm)
    send(sec(0, 1), 1, xp)
    send(sec(0, 3), 0, xm)
    need(0, 3, 1)
    send(sec(0, 3), 1, xp)
    send(sec(0, 3), 1, xm)
    need(0, 1, 0)
    send(sec(0, 1), 0, xp)
    send(sec(0, 1), 0, xm)
    need(3, 3, 0)
    send(sec(3, 3), 0, xp)
    need(1, 1, 1)
    send(sec(1, 1), 1, xm)
    need(0, 2, 0)
    send(sec(0, 2), 0, xp)
    send(sec(0, 2), 0, xm)
    need(0, 2, 1)
    send(sec(0, 2), 1, xm)
    send(sec(0, 2), 1, xp)
    need(1, 3, 1)
    send(sec(1, 3), 1, xm)
    need(3, 1, 0)
    send(sec(3, 1), 0, xp)
    need(3, 2, 0)
    send(sec(3, 2), 0, xp)
    need(1, 2, 1)
    send(sec(1, 2), 1, xm)
    for dx in range(4):
        for dz in range(4):
            for h in range(2):
                if (dx, dz) != (0, 0):
                    need(dx, dz, h)
    keep.wait()
    for copy in sends:
        copy.wait_send()


def tiles_kernel(
    rows_ref, cols_ref, counts_ref, pieces_ref, values_ref, out_ref, held, total, sems
):
    sections, caps = rows_ref.shape
    tile = total.shape[1]
    tile_rows = total.shape[0] - 1
    loads = []
    for t in range(sections):
        loads.append(pltpu.make_async_copy(values_ref.at[t], held.at[t], sems.at[t]))
        loads[-1].start()
    total[...] = jnp.zeros_like(total)

    def body(t, carry):
        pltpu.make_async_copy(values_ref.at[t], held.at[t], sems.at[t]).wait()
        right = jnp.concatenate([pieces_ref[t, 0:tile, :], pieces_ref[t, tile : 2 * tile, :]], axis=1)
        left = held[t].reshape(caps * tile, tile)
        both = jnp.dot(left, right, preferred_element_type=jnp.float32)
        for k in range(caps):
            row = jnp.where(k < counts_ref[t], rows_ref[t, k], tile_rows)
            part = both[k * tile : (k + 1) * tile, :]
            total[row] += jnp.where(cols_ref[t, k] == 0, part[:, :tile], part[:, tile:])
        return carry

    lax.fori_loop(0, sections, body, 0)
    for core in range(2):
        for y in range(8):
            for z in range(2):
                for h in range(2):
                    out_ref[core, y, z, h] = total[((z * 8 + y) * 2 + core) * 2 + h].astype(
                        out_ref.dtype
                    )


def scatter_kernel(
    part_ref, out_ref, mate, first, runs, zout, zin,
    mate_send, mate_recv, run_send, run_recv, z_send, z_recv,
):
    me = lax.axis_index("rep")
    core, y, z = me % 2, (me // 2) % 8, me // 16
    tile = out_ref.shape[0] // 2

    def rep(zz, yy, cc):
        return (zz * 8 + yy % 8) * 2 + cc

    other = rep(z, y, 1 - core)
    steps = (rep(z, y + 1, core), rep(z, y + 7, core))
    across = rep(1 - z, y, core)
    meet("rep", (other, steps[0], steps[1], across))

    swaps = {}
    for dy in (4, 3, 5, 2, 6, 1, 7, 0):
        at = (y + dy) % 8
        swaps[dy] = pltpu.make_async_remote_copy(
            src_ref=part_ref.at[1 - core, at],
            dst_ref=mate.at[at],
            send_sem=mate_send.at[dy],
            recv_sem=mate_recv.at[dy],
            device_id={"rep": other},
            device_id_type=MESH,
        )
        swaps[dy].start()
    swapped = set()

    def term(dy, zi, h):
        dy = dy % 8
        if dy not in swapped:
            swapped.add(dy)
            swaps[dy].wait_recv()
        at = (y + dy) % 8
        zz = 1 - z if zi == 0 else z
        return part_ref[core, at, zz, h].astype(jnp.float32) + mate[at, zz, h].astype(jnp.float32)

    def hops(d, h):
        return 4 if d != h else 3

    copies = {}
    for s in range(4):
        for zi in range(2):
            for d, h in ((0, 1), (1, 0), (0, 0), (1, 1)):
                length = hops(d, h)
                if s >= length:
                    continue
                dy = (length - s) * (1 - 2 * d)
                value = term(dy, zi, h)
                if s == 0:
                    buf = first.at[d, h, zi]
                else:
                    copies[d, h, zi, s - 1].wait_recv()
                    buf = runs.at[d, h, zi, s - 1]
                    value = value + buf[...].astype(jnp.float32)
                buf[...] = value.astype(jnp.bfloat16)
                copies[d, h, zi, s] = pltpu.make_async_remote_copy(
                    src_ref=buf,
                    dst_ref=runs.at[d, h, zi, s],
                    send_sem=run_send.at[d, h, zi, s],
                    recv_sem=run_recv.at[d, h, zi, s],
                    device_id={"rep": steps[d]},
                    device_id_type=MESH,
                )
                copies[d, h, zi, s].start()

    def gathered(zi, h):
        value = term(0, zi, h)
        for d in range(2):
            last = hops(d, h) - 1
            copies[d, h, zi, last].wait_recv()
            value = value + runs[d, h, zi, last].astype(jnp.float32)
        return value

    crosses = []
    for h in range(2):
        zout[h] = gathered(0, h).astype(jnp.bfloat16)
        crosses.append(
            pltpu.make_async_remote_copy(
                src_ref=zout.at[h],
                dst_ref=zin.at[h],
                send_sem=z_send.at[h],
                recv_sem=z_recv.at[h],
                device_id={"rep": across},
                device_id_type=MESH,
            )
        )
        crosses[h].start()
    mine = [gathered(1, h) for h in range(2)]
    for h in range(2):
        crosses[h].wait_recv()
        out_ref[h * tile : (h + 1) * tile, :] = mine[h] + zin[h].astype(jnp.float32)
    for copy in list(swaps.values()) + list(copies.values()) + crosses:
        copy.wait_send()


def shards(
    features, inv_degree, weight, bias_vector, tile_values, tile_rows, tile_cols, tile_counts
):
    rows_dev, width = features.shape
    sections, caps, tile = tile_values.shape[1:4]
    vmem = pl.BlockSpec(memory_space=pltpu.VMEM)
    smem = pl.BlockSpec(memory_space=pltpu.SMEM)
    bf16, f32 = jnp.bfloat16, jnp.float32
    dma = pltpu.SemaphoreType.DMA
    scaled = (inv_degree[:, None] * features.astype(f32)).astype(bf16)
    pieces = pl.pallas_call(
        gather_kernel,
        out_shape=jax.ShapeDtypeStruct((16, rows_dev, width), bf16),
        in_specs=[vmem],
        out_specs=vmem,
        scratch_shapes=[dma((30,)), dma((16, 2)), dma],
        compiler_params=pltpu.CompilerParams(
            collective_id=0, has_side_effects=True, vmem_limit_bytes=VMEM_LIMIT
        ),
        name="gather_pieces",
    )(scaled)
    partial = pl.pallas_call(
        tiles_kernel,
        out_shape=jax.ShapeDtypeStruct((2, 8, 2, 2, tile, width), bf16),
        in_specs=[smem, smem, smem, vmem, pl.BlockSpec(memory_space=pl.ANY)],
        out_specs=vmem,
        scratch_shapes=[
            pltpu.VMEM((sections, caps, tile, tile), bf16),
            pltpu.VMEM((65, tile, width), f32),
            dma((sections,)),
        ],
        compiler_params=pltpu.CompilerParams(vmem_limit_bytes=VMEM_LIMIT),
        name="tile_products",
    )(tile_rows[0], tile_cols[0], tile_counts[0], pieces, tile_values[0])
    summed = pl.pallas_call(
        scatter_kernel,
        out_shape=jax.ShapeDtypeStruct((rows_dev, width), f32),
        in_specs=[vmem],
        out_specs=vmem,
        scratch_shapes=[
            pltpu.VMEM((8, 2, 2, tile, width), bf16),
            pltpu.VMEM((2, 2, 2, tile, width), bf16),
            pltpu.VMEM((2, 2, 2, 4, tile, width), bf16),
            pltpu.VMEM((2, tile, width), bf16),
            pltpu.VMEM((2, tile, width), bf16),
            dma((8,)),
            dma((8,)),
            dma((2, 2, 2, 4)),
            dma((2, 2, 2, 4)),
            dma((2,)),
            dma((2,)),
        ],
        compiler_params=pltpu.CompilerParams(
            collective_id=1, has_side_effects=True, vmem_limit_bytes=VMEM_LIMIT
        ),
        name="scatter_sums",
    )(partial)
    normed = (inv_degree[:, None] * summed).astype(bf16)
    hidden = jnp.dot(normed, weight, preferred_element_type=f32) + bias_vector
    return jnp.maximum(hidden, 0.0).astype(bf16)


def solution(mesh):
    return jax.shard_map(
        shards,
        mesh=mesh,
        in_specs=(
            P(("section", "rep"), None),
            P(("section", "rep")),
            P(),
            P(),
            P(("section", "rep"), None, None, None, None),
            P(("section", "rep"), None, None),
            P(("section", "rep"), None, None),
            P(("section", "rep"), None),
        ),
        out_specs=P(("section", "rep"), None),
        check_vma=False,
    )
```

time: 259 us -> 68.8 us (0.27)
  waiting for transfers between devices: 183 us -> 0 us
  Pallas kernels: 0 us -> 61.7 us
  other arithmetic: 33.5 us -> 1.57 us
  local copies, waits for them, and re-layouts: 16.8 us -> 2.72 us
  between operations: 13.4 us -> 0.07 us
  matrix products: 11.5 us -> 1.76 us
    reduce_scatter x1 -> x0, waiting for transfers between devices: 121 us -> none  [shards(): lax.psum_scatter(flat_partial.astype(jnp.bfloat16), 'rep', scatter_dimens...]
    all_gather x1 -> x0, waiting for transfers between devices: 62.4 us -> none  [shards(): gathered = lax.all_gather(scaled, 'section', axis=0, tiled=True)]
    pallas_call x0 -> x3, Pallas kernels: none -> 61.7 us  [the longest x1 26.5 us: shards(): pl.pallas_call(gather_kernel, out_shape=jax.ShapeDtypeStruct((16, rows_de...]
    scatter-add x1 -> x0, other arithmetic: 26.6 us -> none  [section_terms(): partial_value.at[slot_rows.reshape(-1)]]
    dot_general x2 -> x1, matrix products: 11.5 us -> 1.76 us  [shards(): hidden = jnp.dot(normed, weight, preferred_element_type=f32) + bias_vector]
    reshape x1 -> x0, local copies, waits for them, and re-layouts: 9 us -> none  [section_terms(): products.reshape(groups * slot_count, products.shape[2], products.shape[3])]
    gather x1 -> x0, local copies, waits for them, and re-layouts: 4.29 us -> none  [section_terms(): sources = pieces[section_ids, slot_cols]]
    convert_element_type x2 -> x1, other arithmetic: 5.51 us -> 1.57 us  [shards(): scaled = (inv_degree[:, None] * features.astype(f32)).astype(bf16)]
  transfers between devices with their start and end apart: 2 -> 0, of which waited for: 2 -> 0; matrix products, arithmetic and copies ran while one was open for 1% -> 0% of each run, Pallas kernels for 0% -> 0%
where the time goes in v1:
time: 68.8 us; the launch traced here: 67.9 us
  Pallas kernels  61.7 us (90%)
  local copies, waits for them, and re-layouts  2.72 us (4%)
  matrix products  1.76 us (3%)
  other arithmetic  1.57 us (2%)
    pallas_call x1, Pallas kernels, shards(): pl.pallas_call(gather_kernel, out_shape=jax.ShapeDtypeStruct((16, rows_de...  26.5 us
    pallas_call x1, Pallas kernels, shards(): pl.pallas_call(scatter_kernel, out_shape=jax.ShapeDtypeStruct((rows_dev,...  26.3 us
    pallas_call x1, Pallas kernels, shards(): pl.pallas_call(tiles_kernel, out_shape=jax.ShapeDtypeStruct((2, 8, 2, 2,...  8.94 us
    dot_general x1, matrix products, shards(): hidden = jnp.dot(normed, weight, preferred_element_type=f32) + bias_vector  1.76 us
    convert_element_type x1, other arithmetic, shards(): scaled = (inv_degree[:, None] * features.astype(f32)).astype(bf16)  1.57 us

profile of v1, /device:TPU:6, one launch (start us, length us, event | category | flops | bytes accessed | tf_op | source)
XLA Modules:
  0.0 67.9 jit_solution(14137779468313331984)
XLA Ops:
  0.0 0.0 copy-start
  0.0 1.4 %copy.9.rows_ref = s32[16,8]{1,0:T(8,128)} copy(s32[16,8]{0,1:T(8,128)} %bitcast.6) | data formatting | bytes 1024 | tf_op jit(solution)/shard_map/squeeze | solution.py:275
  1.4 1.4 %copy.10.cols_ref = s32[16,8]{1,0:T(8,128)} copy(s32[16,8]{0,1:T(8,128)} %bitcast.7) | data formatting | bytes 1024 | tf_op jit(solution)/shard_map/squeeze | solution.py:275
  2.7 1.6 %multiply_convert_fusion.1.own_ref = bf16[256,128]{1,0:T(8,128)(2,1)} fusion(bf16[256,128]{1,0:T(8,128)(2,1)} %param.8, f32[256]{0:T(256)} %param.9), kind=kLoop, calls=%fused_computation.4 | loop fusion | flops 98304 | bytes 132096 | tf_op jit(solution)/shard_map/convert_element_type | solution.py:251
  4.3 26.5 %gather_pieces.1.pieces_ref = bf16[16,256,128]{2,1,0:T(8,128)(2,1)} custom-call(bf16[256,128]{1,0:T(8,128)(2,1)} %multiply_convert_fusion.1.own_ref), custom_call_target="tpu_custom_call" | custom-call | tf_op jit(solution)/shard_map/gather_pieces/pallas_call | solution.py:252
  30.8 0.0 copy-start.1
  30.8 0.0 copy-start.2
  30.8 8.9 %tile_products.1.part_ref = bf16[2,8,2,2,128,128]{5,4,3,2,1,0:T(8,128)(2,1)} custom-call(s32[16,8]{1,0:T(8,128)} %copy.9.rows_ref, s32[16,8]{1,0:T(8,128)} %copy.10.cols_ref, s32[16]{0:T(128)} %bitcast.8, bf16[16,256,128]{2,1,0:T(8,128)(2,1)} %gather_pieces.1.pieces_ref, bf16[16,8,128,128]{3,2,1,0:T(8,128)(2,1)} %bitcast.5), custom_call_target="tpu_custom_call" | custom-call | tf_op jit(solution)/shard_map/tile_products/pallas_call | solution.py:263
  39.7 26.3 %scatter_sums.1 = f32[256,128]{1,0:T(8,128)} custom-call(bf16[2,8,2,2,128,128]{5,4,3,2,1,0:T(8,128)(2,1)} %tile_products.1.part_ref), custom_call_target="tpu_custom_call" | custom-call | tf_op jit(solution)/shard_map/scatter_sums/pallas_call | solution.py:276
  66.1 0.0 copy-done
  66.1 0.0 copy-done.1
  66.1 0.0 copy-done.2
  66.1 1.8 %fusion.1 = bf16[256,128]{1,0:T(8,128)(2,1)} fusion(bf16[128,128]{1,0:T(8,128)(2,1)S(1)} %copy-done, f32[256,128]{1,0:T(8,128)} %scatter_sums.1, f32[128]{0:T(128)S(1)} %copy-done.2, f32[256]{0:T(256)S(1)} %copy-done.1), kind=kOutput, calls=%fused_computation.2 | convolution fusion | flops 8552448 | bytes 230912 | tf_op jit(solution)/shard_map/dot_general | solution.py:300
Async XLA Ops:
  0.0 66.1 %copy-start = (bf16[128,128]{1,0:T(8,128)(2,1)S(1)}, bf16[128,128]{1,0:T(8,128)(2,1)}, u32[]{:S(2)}) copy-start(bf16[128,128]{1,0:T(8,128)(2,1)} %param.10) | copy-start | bytes 98308
  30.8 35.3 %copy-start.1 = (f32[256]{0:T(256)S(1)}, f32[256]{0:T(256)}, u32[]{:S(2)}) copy-start(f32[256]{0:T(256)} %param.9) | copy-start | bytes 3076
  30.8 35.3 %copy-start.2 = (f32[128]{0:T(128)S(1)}, f32[128]{0:T(128)}, u32[]{:S(2)}) copy-start(f32[128]{0:T(128)} %param.11) | copy-start | bytes 1540

commit v2 on v1

--- a/solution.py
+++ b/solution.py
@@ -6,32 +6,55 @@
 from jax.sharding import PartitionSpec as P
 
 MESH = pl.DeviceIdType.MESH
-VMEM_LIMIT = 60 * 1024 * 1024
-
-
-def meet(axis, peers):
+MIB = 1024 * 1024
+
+
+def greet(axis, peers):
     barrier = pltpu.get_barrier_semaphore()
     for peer in peers:
         pl.semaphore_signal(barrier, inc=1, device_id={axis: peer}, device_id_type=MESH)
-    pl.semaphore_wait(barrier, len(peers))
-
-
-def gather_kernel(own_ref, out_ref, send_sems, recv_sems, local_sem):
+    return lambda: pl.semaphore_wait(barrier, len(peers))
+
+
+def gather_kernel(
+    features_hbm, inv_hbm, values_hbm, out_ref, values_ref,
+    features_ref, inv_ref, send_sems, recv_sems, load_sems, value_sems,
+):
     me = lax.axis_index("section")
     x, z = me // 4, me % 4
-    half = own_ref.shape[0] // 2
+    half = features_ref.shape[0] // 2
 
     def sec(dx, dz):
         return ((x + dx) % 4) * 4 + (z + dz) % 4
 
     zp, zm, xp, xm = sec(0, 1), sec(0, 3), sec(1, 0), sec(3, 0)
-    meet("section", (zp, zm, xp, xm))
+    met = greet("section", (zp, zm, xp, xm))
+    loads = [
+        pltpu.make_async_copy(features_hbm, features_ref, load_sems.at[0]),
+        pltpu.make_async_copy(inv_hbm, inv_ref, load_sems.at[1]),
+    ]
+    for load in loads:
+        load.start()
+    fills = [
+        pltpu.make_async_copy(values_hbm.at[t], values_ref.at[t], value_sems.at[t])
+        for t in range(values_ref.shape[0])
+    ]
+    for load in loads:
+        load.wait()
+    for fill in fills:
+        fill.start()
+    for h in range(2):
+        rows = slice(h * half, (h + 1) * half)
+        column = jnp.transpose(jnp.broadcast_to(inv_ref[h : h + 1, :], (half, half)))
+        scaled = column * features_ref[rows, :].astype(jnp.float32)
+        out_ref[me, rows, :] = scaled.astype(out_ref.dtype)
+    met()
     sends = []
 
-    def send(slot, h, peer, own=False):
+    def send(slot, h, peer):
         rows = pl.ds(h * half, half)
         copy = pltpu.make_async_remote_copy(
-            src_ref=own_ref.at[rows] if own else out_ref.at[slot, rows],
+            src_ref=out_ref.at[slot, rows],
             dst_ref=out_ref.at[slot, rows],
             send_sem=send_sems.at[len(sends)],
             recv_sem=recv_sems.at[slot, h],
@@ -58,9 +81,7 @@
         ).wait_recv()
 
     for h, peer in ((0, zp), (1, zm), (1, zp), (0, zm), (0, xp), (1, xm), (1, xp), (0, xm)):
-        send(me, h, peer, own=True)
-    keep = pltpu.make_async_copy(own_ref, out_ref.at[me], local_sem)
-    keep.start()
+        send(me, h, peer)
 
     need(0, 3, 0)
     send(sec(0, 3), 0, zp)
@@ -103,32 +124,39 @@
             for h in range(2):
                 if (dx, dz) != (0, 0):
                     need(dx, dz, h)
-    keep.wait()
+    for fill in fills:
+        fill.wait()
     for copy in sends:
         copy.wait_send()
 
 
 def tiles_kernel(
-    rows_ref, cols_ref, counts_ref, pieces_ref, values_ref, out_ref, held, total, sems
+    rows_hbm, cols_hbm, counts_hbm, pieces_ref, values_ref, out_ref,
+    rows_ref, cols_ref, counts_ref, total, sems,
 ):
-    sections, caps = rows_ref.shape
+    loads = [
+        pltpu.make_async_copy(source, target, sems.at[i])
+        for i, (source, target) in enumerate(
+            ((rows_hbm, rows_ref), (cols_hbm, cols_ref), (counts_hbm, counts_ref))
+        )
+    ]
+    for load in loads:
+        load.start()
+    caps, sections = rows_ref.shape
     tile = total.shape[1]
     tile_rows = total.shape[0] - 1
-    loads = []
-    for t in range(sections):
-        loads.append(pltpu.make_async_copy(values_ref.at[t], held.at[t], sems.at[t]))
-        loads[-1].start()
     total[...] = jnp.zeros_like(total)
+    for load in loads:
+        load.wait()
 
     def body(t, carry):
-        pltpu.make_async_copy(values_ref.at[t], held.at[t], sems.at[t]).wait()
         right = jnp.concatenate([pieces_ref[t, 0:tile, :], pieces_ref[t, tile : 2 * tile, :]], axis=1)
-        left = held[t].reshape(caps * tile, tile)
+        left = values_ref[t].reshape(caps * tile, tile)
         both = jnp.dot(left, right, preferred_element_type=jnp.float32)
         for k in range(caps):
-            row = jnp.where(k < counts_ref[t], rows_ref[t, k], tile_rows)
+            row = jnp.where(k < counts_ref[0, t], rows_ref[k, t], tile_rows)
             part = both[k * tile : (k + 1) * tile, :]
-            total[row] += jnp.where(cols_ref[t, k] == 0, part[:, :tile], part[:, tile:])
+            total[row] += jnp.where(cols_ref[k, t] == 0, part[:, :tile], part[:, tile:])
         return carry
 
     lax.fori_loop(0, sections, body, 0)
@@ -155,7 +183,7 @@
     other = rep(z, y, 1 - core)
     steps = (rep(z, y + 1, core), rep(z, y + 7, core))
     across = rep(1 - z, y, core)
-    meet("rep", (other, steps[0], steps[1], across))
+    greet("rep", (other, steps[0], steps[1], across))()
 
     swaps = {}
     for dy in (4, 3, 5, 2, 6, 1, 7, 0):
@@ -245,34 +273,46 @@
     rows_dev, width = features.shape
     sections, caps, tile = tile_values.shape[1:4]
     vmem = pl.BlockSpec(memory_space=pltpu.VMEM)
-    smem = pl.BlockSpec(memory_space=pltpu.SMEM)
+    hbm = pl.BlockSpec(memory_space=pltpu.HBM)
     bf16, f32 = jnp.bfloat16, jnp.float32
     dma = pltpu.SemaphoreType.DMA
-    scaled = (inv_degree[:, None] * features.astype(f32)).astype(bf16)
-    pieces = pl.pallas_call(
+    pieces, values = pl.pallas_call(
         gather_kernel,
-        out_shape=jax.ShapeDtypeStruct((16, rows_dev, width), bf16),
-        in_specs=[vmem],
-        out_specs=vmem,
-        scratch_shapes=[dma((30,)), dma((16, 2)), dma],
+        out_shape=(
+            pltpu.VMEM((16, rows_dev, width), bf16),
+            pltpu.VMEM(tile_values.shape[1:], bf16),
+        ),
+        in_specs=[hbm, hbm, hbm],
+        out_specs=(vmem, vmem),
+        scratch_shapes=[
+            pltpu.VMEM((rows_dev, width), bf16),
+            pltpu.VMEM((2, rows_dev // 2), f32),
+            dma((30,)),
+            dma((16, 2)),
+            dma((2,)),
+            dma((sections,)),
+        ],
         compiler_params=pltpu.CompilerParams(
-            collective_id=0, has_side_effects=True, vmem_limit_bytes=VMEM_LIMIT
+            collective_id=0, has_side_effects=True, vmem_limit_bytes=57 * MIB
         ),
+        cost_estimate=pl.CostEstimate(flops=0, bytes_accessed=48 * MIB, transcendentals=0),
         name="gather_pieces",
-    )(scaled)
+    )(features, inv_degree.reshape(2, rows_dev // 2), tile_values[0])
     partial = pl.pallas_call(
         tiles_kernel,
         out_shape=jax.ShapeDtypeStruct((2, 8, 2, 2, tile, width), bf16),
-        in_specs=[smem, smem, smem, vmem, pl.BlockSpec(memory_space=pl.ANY)],
+        in_specs=[hbm, hbm, hbm, vmem, vmem],
         out_specs=vmem,
         scratch_shapes=[
-            pltpu.VMEM((sections, caps, tile, tile), bf16),
+            pltpu.SMEM((caps, sections), jnp.int32),
+            pltpu.SMEM((caps, sections), jnp.int32),
+            pltpu.SMEM((1, sections), jnp.int32),
             pltpu.VMEM((65, tile, width), f32),
-            dma((sections,)),
+            dma((3,)),
         ],
-        compiler_params=pltpu.CompilerParams(vmem_limit_bytes=VMEM_LIMIT),
+        compiler_params=pltpu.CompilerParams(vmem_limit_bytes=20 * MIB),
         name="tile_products",
-    )(tile_rows[0], tile_cols[0], tile_counts[0], pieces, tile_values[0])
+    )(tile_rows[0].T, tile_cols[0].T, tile_counts, pieces, values)
     summed = pl.pallas_call(
         scatter_kernel,
         out_shape=jax.ShapeDtypeStruct((rows_dev, width), f32),
@@ -292,8 +332,9 @@
             dma((2,)),
         ],
         compiler_params=pltpu.CompilerParams(
-            collective_id=1, has_side_effects=True, vmem_limit_bytes=VMEM_LIMIT
+            collective_id=1, has_side_effects=True, vmem_limit_bytes=16 * MIB
         ),
+        cost_estimate=pl.CostEstimate(flops=0, bytes_accessed=48 * MIB, transcendentals=0),
         name="scatter_sums",
     )(partial)
     normed = (inv_degree[:, None] * summed).astype(bf16)

time: 68.8 us -> 56.1 us (0.82); the launches traced: 67.9 us -> 55.9 us
  Pallas kernels: 61.7 us -> 54.9 us
  local copies, waits for them, and re-layouts: 2.72 us -> 0.03 us
  other arithmetic: 1.57 us -> 0 us
  matrix products: 1.76 us -> 0.86 us
    pallas_call x1, Pallas kernels: 8.94 us -> 5.83 us  [shards(): pl.pallas_call(tiles_kernel, out_shape=jax.ShapeDtypeStruct((2, 8, 2, 2,...]
    squeeze x2 -> x0, local copies, waits for them, and re-layouts: 2.71 us -> none  [the longest x1 1.36 us: shards(): tile_rows[0]]
    pallas_call x1, Pallas kernels: 26.3 us -> 24.3 us  [shards(): pl.pallas_call(scatter_kernel, out_shape=jax.ShapeDtypeStruct((rows_dev,...]
    pallas_call x1, Pallas kernels: 26.5 us -> 24.8 us  [shards(): pl.pallas_call(gather_kernel, out_shape=(pltpu.VMEM((16, rows_dev, width)...]
    convert_element_type x1 -> x0, other arithmetic: 1.57 us -> none  [shards(): scaled = (inv_degree[:, None] * features.astype(f32)).astype(bf16)]
    dot_general x1, matrix products: 1.76 us -> 0.86 us  [shards(): hidden = jnp.dot(normed, weight, preferred_element_type=f32) + bias_vector]
where the time goes in v2:
time: 56.1 us; the launch traced here: 55.9 us
  Pallas kernels  54.9 us (98%)
  matrix products  0.86 us (2%)
    pallas_call x1, Pallas kernels, shards(): pl.pallas_call(gather_kernel, out_shape=(pltpu.VMEM((16, rows_dev, width)...  24.8 us
    pallas_call x1, Pallas kernels, shards(): pl.pallas_call(scatter_kernel, out_shape=jax.ShapeDtypeStruct((rows_dev,...  24.3 us
    pallas_call x1, Pallas kernels, shards(): pl.pallas_call(tiles_kernel, out_shape=jax.ShapeDtypeStruct((2, 8, 2, 2,...  5.83 us

profile of v2, /device:TPU:6, one launch (start us, length us, event | category | flops | bytes accessed | tf_op | source)
XLA Modules:
  0.0 55.9 jit_solution(219824614798969035)
XLA Ops:
  0.0 0.0 copy-start
  0.0 0.0 copy-start.3
  0.0 0.0 copy-start.2
  0.0 0.0 copy-start.1
  0.0 24.8 %gather_pieces.1 = (bf16[16,256,128]{2,1,0:T(8,128)(2,1)S(1)}, bf16[16,8,128,128]{3,2,1,0:T(8,128)(2,1)S(1)}) custom-call(bf16[256,128]{1,0:T(8,128)(2,1)} %features_hbm.1, f32[2,128]{1,0:T(2,128)} %bitcast.12, bf16[16,8,128,128]{3,2,1,0:T(8,128)(2,1)} %bitcast.11), custom_call_target="tpu_custom_call" | custom-call | bytes 50331648 | tf_op jit(solution)/shard_map/gather_pieces/pallas_call | solution.py:279
  24.8 0.0 copy-done.3
  24.8 0.0 copy-done.2
  24.8 0.0 copy-done.1
  24.8 0.0 copy-start.4
  24.8 0.0 copy-start.5
  24.9 5.8 %tile_products.1.part_ref = bf16[2,8,2,2,128,128]{5,4,3,2,1,0:T(8,128)(2,1)S(1)} custom-call(s32[8,16]{1,0:T(8,128)S(1)} %bitcast.9, s32[8,16]{1,0:T(8,128)S(1)} %bitcast.10, s32[1,16]{1,0:T(1,128)S(1)} %copy-done.3, bf16[16,256,128]{2,1,0:T(8,128)(2,1)S(1)} %get-tuple-element.7.pieces_ref, bf16[16,8,128,128]{3,2,1,0:T(8,128)(2,1)S(1)} %get-tuple-element.8.values_ref), custom_call_target="tpu_custom_call" | custom-call | tf_op jit(solution)/shard_map/tile_products/pallas_call | solution.py:301
  30.7 24.3 %scatter_sums.1 = f32[256,128]{1,0:T(8,128)S(1)} custom-call(bf16[2,8,2,2,128,128]{5,4,3,2,1,0:T(8,128)(2,1)S(1)} %tile_products.1.part_ref), custom_call_target="tpu_custom_call" | custom-call | bytes 50331648 | tf_op jit(solution)/shard_map/scatter_sums/pallas_call | solution.py:316
  55.0 0.0 copy-done
  55.0 0.0 copy-done.4
  55.0 0.0 copy-done.5
  55.0 0.9 %fusion.1 = bf16[256,128]{1,0:T(8,128)(2,1)} fusion(bf16[128,128]{1,0:T(8,128)(2,1)S(1)} %copy-done, f32[256,128]{1,0:T(8,128)S(1)} %scatter_sums.1, f32[128]{0:T(128)S(1)} %copy-done.5, f32[256]{0:T(256)S(1)} %copy-done.4), kind=kOutput, calls=%fused_computation.2 | convolution fusion | flops 8552448 | bytes 230912 | tf_op jit(solution)/shard_map/dot_general | solution.py:341
Async XLA Ops:
  0.0 55.0 %copy-start = (bf16[128,128]{1,0:T(8,128)(2,1)S(1)}, bf16[128,128]{1,0:T(8,128)(2,1)}, u32[]{:S(2)}) copy-start(bf16[128,128]{1,0:T(8,128)(2,1)} %param.10) | copy-start | bytes 98308
  0.0 24.8 %copy-start.3 = (s32[1,16]{1,0:T(1,128)S(1)}, s32[1,16]{1,0:T(1,128)}, u32[]{:S(2)}) copy-start(s32[1,16]{1,0:T(1,128)} %counts_hbm.1) | copy-start | bytes 196
  0.0 24.8 %copy-start.2 = (s32[1,16,8]{1,2,0:T(8,128)S(1)}, s32[1,16,8]{1,2,0:T(8,128)}, u32[]{:S(2)}) copy-start(s32[1,16,8]{1,2,0:T(8,128)} %param.14) | copy-start | bytes 1540
  0.0 24.8 %copy-start.1 = (s32[1,16,8]{1,2,0:T(8,128)S(1)}, s32[1,16,8]{1,2,0:T(8,128)}, u32[]{:S(2)}) copy-start(s32[1,16,8]{1,2,0:T(8,128)} %param.13) | copy-start | bytes 1540
  24.8 30.2 %copy-start.4 = (f32[256]{0:T(256)S(1)}, f32[256]{0:T(256)}, u32[]{:S(2)}) copy-start(f32[256]{0:T(256)} %param.9) | copy-start | bytes 3076
  24.8 30.2 %copy-start.5 = (f32[128]{0:T(128)S(1)}, f32[128]{0:T(128)}, u32[]{:S(2)}) copy-start(f32[128]{0:T(128)} %param.11) | copy-start | bytes 1540

commit v3 on v2

--- a/solution.py
+++ b/solution.py
@@ -7,6 +7,7 @@
 
 MESH = pl.DeviceIdType.MESH
 MIB = 1024 * 1024
+PARTS = ((0, 96, "zx", 0), (96, 96, "zx", 1), (192, 32, "xz", 0), (224, 32, "xz", 1))
 
 
 def greet(axis, peers):
@@ -50,80 +51,55 @@
         out_ref[me, rows, :] = scaled.astype(out_ref.dtype)
     met()
     sends = []
-
-    def send(slot, h, peer):
-        rows = pl.ds(h * half, half)
-        copy = pltpu.make_async_remote_copy(
-            src_ref=out_ref.at[slot, rows],
-            dst_ref=out_ref.at[slot, rows],
-            send_sem=send_sems.at[len(sends)],
-            recv_sem=recv_sems.at[slot, h],
+    neighbours = {"z": (zp, zm), "x": (xp, xm)}
+
+    def rows_of(part):
+        return pl.ds(PARTS[part][0], PARTS[part][1])
+
+    def remote(slot, part, peer, n):
+        return pltpu.make_async_remote_copy(
+            src_ref=out_ref.at[slot, rows_of(part)],
+            dst_ref=out_ref.at[slot, rows_of(part)],
+            send_sem=send_sems.at[n],
+            recv_sem=recv_sems.at[slot, part],
             device_id={"section": peer},
             device_id_type=MESH,
         )
-        copy.start()
-        sends.append(copy)
-
-    waited = set()
-
-    def need(dx, dz, h):
-        if (dx, dz, h) in waited:
-            return
-        waited.add((dx, dz, h))
-        slot, rows = sec(dx, dz), pl.ds(h * half, half)
-        pltpu.make_async_remote_copy(
-            src_ref=out_ref.at[slot, rows],
-            dst_ref=out_ref.at[slot, rows],
-            send_sem=send_sems.at[0],
-            recv_sem=recv_sems.at[slot, h],
-            device_id={"section": zp},
-            device_id_type=MESH,
-        ).wait_recv()
-
-    for h, peer in ((0, zp), (1, zm), (1, zp), (0, zm), (0, xp), (1, xm), (1, xp), (0, xm)):
-        send(me, h, peer)
-
-    need(0, 3, 0)
-    send(sec(0, 3), 0, zp)
-    need(0, 1, 1)
-    send(sec(0, 1), 1, zm)
-    send(sec(0, 3), 0, xp)
-    send(sec(0, 1), 1, xm)
-    need(3, 0, 0)
-    send(sec(3, 0), 0, xp)
-    need(1, 0, 1)
-    send(sec(1, 0), 1, xm)
-    send(sec(0, 1), 1, xp)
-    send(sec(0, 3), 0, xm)
-    need(0, 3, 1)
-    send(sec(0, 3), 1, xp)
-    send(sec(0, 3), 1, xm)
-    need(0, 1, 0)
-    send(sec(0, 1), 0, xp)
-    send(sec(0, 1), 0, xm)
-    need(3, 3, 0)
-    send(sec(3, 3), 0, xp)
-    need(1, 1, 1)
-    send(sec(1, 1), 1, xm)
-    need(0, 2, 0)
-    send(sec(0, 2), 0, xp)
-    send(sec(0, 2), 0, xm)
-    need(0, 2, 1)
-    send(sec(0, 2), 1, xm)
-    send(sec(0, 2), 1, xp)
-    need(1, 3, 1)
-    send(sec(1, 3), 1, xm)
-    need(3, 1, 0)
-    send(sec(3, 1), 0, xp)
-    need(3, 2, 0)
-    send(sec(3, 2), 0, xp)
-    need(1, 2, 1)
-    send(sec(1, 2), 1, xm)
-    for dx in range(4):
-        for dz in range(4):
-            for h in range(2):
-                if (dx, dz) != (0, 0):
-                    need(dx, dz, h)
+
+    def send(slot, part, axis, way):
+        sends.append(remote(slot, part, neighbours[axis][way], len(sends)))
+        sends[-1].start()
+
+    for turn in range(2):
+        for part in range(4):
+            axis = PARTS[part][2][turn]
+            for way in ((0, 1), (1, 0))[PARTS[part][3]]:
+                send(me, part, axis, way)
+
+    def when(item):
+        part, dx, dz = item
+        x_hops, z_hops = min(dx, 4 - dx), min(dz, 4 - dz)
+        if PARTS[part][2] == "zx":
+            return 3.6 * z_hops + 2.4 * x_hops, part
+        return 2.0 * x_hops + 3.4 * z_hops, part
+
+    items = [
+        (part, dx, dz) for part in range(4) for dx in range(4) for dz in range(4) if dx or dz
+    ]
+    for part, dx, dz in sorted(items, key=when):
+        slot = sec(dx, dz)
+        remote(slot, part, zp, 0).wait_recv()
+        early, late = PARTS[part][2]
+        way = PARTS[part][3]
+        moved = {"x": dx, "z": dz}
+        source = (3, 1)[way]
+        if moved[late] == 0:
+            if moved[early] == source:
+                send(slot, part, early, way)
+            send(slot, part, late, way)
+            send(slot, part, late, 1 - way)
+        elif moved[late] == source:
+            send(slot, part, late, way)
     for fill in fills:
         fill.wait()
     for copy in sends:
@@ -170,12 +146,13 @@
 
 
 def scatter_kernel(
-    part_ref, out_ref, mate, first, runs, zout, zin,
-    mate_send, mate_recv, run_send, run_recv, z_send, z_recv,
+    part_ref, out_ref, mate, first0, runs0, first1, runs1, zout, zin,
+    mate_send, mate_recv, send0, recv0, send1, recv1, z_send, z_recv,
 ):
     me = lax.axis_index("rep")
     core, y, z = me % 2, (me // 2) % 8, me // 16
     tile = out_ref.shape[0] // 2
+    f32, bf16 = jnp.float32, jnp.bfloat16
 
     def rep(zz, yy, cc):
         return (zz * 8 + yy % 8) * 2 + cc
@@ -184,20 +161,28 @@
     steps = (rep(z, y + 1, core), rep(z, y + 7, core))
     across = rep(1 - z, y, core)
     greet("rep", (other, steps[0], steps[1], across))()
-
-    swaps = {}
-    for dy in (4, 3, 5, 2, 6, 1, 7, 0):
-        at = (y + dy) % 8
-        swaps[dy] = pltpu.make_async_remote_copy(
-            src_ref=part_ref.at[1 - core, at],
-            dst_ref=mate.at[at],
-            send_sem=mate_send.at[dy],
-            recv_sem=mate_recv.at[dy],
-            device_id={"rep": other},
+    started = []
+
+    def send(source, target, send_sem, recv_sem, peer):
+        copy = pltpu.make_async_remote_copy(
+            src_ref=source,
+            dst_ref=target,
+            send_sem=send_sem,
+            recv_sem=recv_sem,
+            device_id={"rep": peer},
             device_id_type=MESH,
         )
-        swaps[dy].start()
-    swapped = set()
+        copy.start()
+        started.append(copy)
+        return copy
+
+    order = (4, 3, 5, 2, 6, 1, 7, 0)
+    swaps, swapped = {}, set()
+    for dy in order:
+        at = (y + dy) % 8
+        swaps[dy] = send(
+            part_ref.at[1 - core, at], mate.at[at], mate_send.at[dy], mate_recv.at[dy], other
+        )
 
     def term(dy, zi, h):
         dy = dy % 8
@@ -206,64 +191,84 @@
             swaps[dy].wait_recv()
         at = (y + dy) % 8
         zz = 1 - z if zi == 0 else z
-        return part_ref[core, at, zz, h].astype(jnp.float32) + mate[at, zz, h].astype(jnp.float32)
-
-    def hops(d, h):
-        return 4 if d != h else 3
+        return part_ref[core, at, zz, h].astype(f32) + mate[at, zz, h].astype(f32)
+
+    crosses = {}
+
+    def cross(dy):
+        zout[dy] = term(dy, 0, 1).astype(bf16)
+        crosses[dy] = send(zout.at[dy], zin.at[dy], z_send.at[dy], z_recv.at[dy], across)
+
+    def term1(dy):
+        dy = dy % 8
+        crosses[dy].wait_recv()
+        return term(dy, 1, 1) + zin[dy].astype(f32)
 
     copies = {}
-    for s in range(4):
+
+    def hop0(d, s):
+        length = 3 + d
         for zi in range(2):
-            for d, h in ((0, 1), (1, 0), (0, 0), (1, 1)):
-                length = hops(d, h)
-                if s >= length:
-                    continue
-                dy = (length - s) * (1 - 2 * d)
-                value = term(dy, zi, h)
-                if s == 0:
-                    buf = first.at[d, h, zi]
-                else:
-                    copies[d, h, zi, s - 1].wait_recv()
-                    buf = runs.at[d, h, zi, s - 1]
-                    value = value + buf[...].astype(jnp.float32)
-                buf[...] = value.astype(jnp.bfloat16)
-                copies[d, h, zi, s] = pltpu.make_async_remote_copy(
-                    src_ref=buf,
-                    dst_ref=runs.at[d, h, zi, s],
-                    send_sem=run_send.at[d, h, zi, s],
-                    recv_sem=run_recv.at[d, h, zi, s],
-                    device_id={"rep": steps[d]},
-                    device_id_type=MESH,
-                )
-                copies[d, h, zi, s].start()
-
-    def gathered(zi, h):
-        value = term(0, zi, h)
+            value = term((length - s) * (1 - 2 * d), zi, 0)
+            if s == 0:
+                buf = first0.at[d, zi]
+            else:
+                copies[0, d, zi, s - 1].wait_recv()
+                buf = runs0.at[d, zi, s - 1]
+                value = value + buf[...].astype(f32)
+            buf[...] = value.astype(bf16)
+            copies[0, d, zi, s] = send(
+                buf, runs0.at[d, zi, s], send0.at[d, zi, s], recv0.at[d, zi, s], steps[d]
+            )
+
+    def hop1(d, s):
+        length = 4 - d
+        value = term1((length - s) * (1 - 2 * d))
+        if s == 0:
+            buf = first1.at[d]
+        else:
+            copies[1, d, s - 1].wait_recv()
+            buf = runs1.at[d, s - 1]
+            value = value + buf[...].astype(f32)
+        buf[...] = value.astype(bf16)
+        copies[1, d, s] = send(buf, runs1.at[d, s], send1.at[d, s], recv1.at[d, s], steps[d])
+
+    hop0(1, 0)
+    cross(4)
+    hop0(0, 0)
+    for dy in order[1:]:
+        cross(dy)
+    hop0(1, 1)
+    hop0(0, 1)
+    hop1(0, 0)
+    hop1(1, 0)
+    hop0(1, 2)
+    hop0(0, 2)
+    hop1(0, 1)
+    hop1(1, 1)
+    hop0(1, 3)
+    hop1(0, 2)
+    hop1(1, 2)
+
+    def gathered0(zi):
+        value = term(0, zi, 0)
         for d in range(2):
-            last = hops(d, h) - 1
-            copies[d, h, zi, last].wait_recv()
-            value = value + runs[d, h, zi, last].astype(jnp.float32)
+            copies[0, d, zi, 2 + d].wait_recv()
+            value = value + runs0[d, zi, 2 + d].astype(f32)
         return value
 
-    crosses = []
-    for h in range(2):
-        zout[h] = gathered(0, h).astype(jnp.bfloat16)
-        crosses.append(
-            pltpu.make_async_remote_copy(
-                src_ref=zout.at[h],
-                dst_ref=zin.at[h],
-                send_sem=z_send.at[h],
-                recv_sem=z_recv.at[h],
-                device_id={"rep": across},
-                device_id_type=MESH,
-            )
-        )
-        crosses[h].start()
-    mine = [gathered(1, h) for h in range(2)]
-    for h in range(2):
-        crosses[h].wait_recv()
-        out_ref[h * tile : (h + 1) * tile, :] = mine[h] + zin[h].astype(jnp.float32)
-    for copy in list(swaps.values()) + list(copies.values()) + crosses:
+    zout[8] = gathered0(0).astype(bf16)
+    last = send(zout.at[8], zin.at[8], z_send.at[8], z_recv.at[8], across)
+    hop1(0, 3)
+    mine = gathered0(1)
+    value = term1(0)
+    for d in range(2):
+        copies[1, d, 3 - d].wait_recv()
+        value = value + runs1[d, 3 - d].astype(f32)
+    out_ref[tile:, :] = value
+    last.wait_recv()
+    out_ref[:tile, :] = mine + zin[8].astype(f32)
+    for copy in started:
         copy.wait_send()
 
 
@@ -287,8 +292,8 @@
         scratch_shapes=[
             pltpu.VMEM((rows_dev, width), bf16),
             pltpu.VMEM((2, rows_dev // 2), f32),
-            dma((30,)),
-            dma((16, 2)),
+            dma((60,)),
+            dma((16, 4)),
             dma((2,)),
             dma((sections,)),
         ],
@@ -320,16 +325,20 @@
         out_specs=vmem,
         scratch_shapes=[
             pltpu.VMEM((8, 2, 2, tile, width), bf16),
-            pltpu.VMEM((2, 2, 2, tile, width), bf16),
-            pltpu.VMEM((2, 2, 2, 4, tile, width), bf16),
+            pltpu.VMEM((2, 2, tile, width), bf16),
+            pltpu.VMEM((2, 2, 4, tile, width), bf16),
             pltpu.VMEM((2, tile, width), bf16),
-            pltpu.VMEM((2, tile, width), bf16),
+            pltpu.VMEM((2, 4, tile, width), bf16),
+            pltpu.VMEM((9, tile, width), bf16),
+            pltpu.VMEM((9, tile, width), bf16),
             dma((8,)),
             dma((8,)),
-            dma((2, 2, 2, 4)),
-            dma((2, 2, 2, 4)),
-            dma((2,)),
-            dma((2,)),
+            dma((2, 2, 4)),
+            dma((2, 2, 4)),
+            dma((2, 4)),
+            dma((2, 4)),
+            dma((9,)),
+            dma((9,)),
         ],
         compiler_params=pltpu.CompilerParams(
             collective_id=1, has_side_effects=True, vmem_limit_bytes=16 * MIB

time: 56.1 us -> 59.3 us (1.057)
  Pallas kernels: 54.9 us -> 58.1 us
    pallas_call x1, Pallas kernels: 24.8 us -> 28.6 us  [shards(): pl.pallas_call(gather_kernel, out_shape=(pltpu.VMEM((16, rows_dev, width)...]
    pallas_call x1, Pallas kernels: 24.3 us -> 23.6 us  [shards(): pl.pallas_call(scatter_kernel, out_shape=jax.ShapeDtypeStruct((rows_dev,...]
where the time goes in v3:
time: 59.3 us; the launch traced here: 59.1 us
  Pallas kernels  58.1 us (98%)
  matrix products  0.86 us (1%)
    pallas_call x1, Pallas kernels, shards(): pl.pallas_call(gather_kernel, out_shape=(pltpu.VMEM((16, rows_dev, width)...  28.6 us
    pallas_call x1, Pallas kernels, shards(): pl.pallas_call(scatter_kernel, out_shape=jax.ShapeDtypeStruct((rows_dev,...  23.6 us
    pallas_call x1, Pallas kernels, shards(): pl.pallas_call(tiles_kernel, out_shape=jax.ShapeDtypeStruct((2, 8, 2, 2,...  5.93 us

profile of v3, /device:TPU:6, one launch (start us, length us, event | category | flops | bytes accessed | tf_op | source)
XLA Modules:
  0.0 59.1 jit_solution(9466533184799767738)
XLA Ops:
  0.0 0.0 copy-start
  0.0 0.0 copy-start.3
  0.0 0.0 copy-start.2
  0.0 0.0 copy-start.1
  0.0 28.6 %gather_pieces.1 = (bf16[16,256,128]{2,1,0:T(8,128)(2,1)S(1)}, bf16[16,8,128,128]{3,2,1,0:T(8,128)(2,1)S(1)}) custom-call(bf16[256,128]{1,0:T(8,128)(2,1)} %features_hbm.1, f32[2,128]{1,0:T(2,128)} %bitcast.12, bf16[16,8,128,128]{3,2,1,0:T(8,128)(2,1)} %bitcast.11), custom_call_target="tpu_custom_call" | custom-call | bytes 50331648 | tf_op jit(solution)/shard_map/gather_pieces/pallas_call | solution.py:284
  28.6 0.0 copy-done.3
  28.6 0.0 copy-done.2
  28.6 0.0 copy-done.1
  28.6 0.0 copy-start.4
  28.7 0.0 copy-start.5
  28.7 5.9 %tile_products.1.part_ref = bf16[2,8,2,2,128,128]{5,4,3,2,1,0:T(8,128)(2,1)S(1)} custom-call(s32[8,16]{1,0:T(8,128)S(1)} %bitcast.9, s32[8,16]{1,0:T(8,128)S(1)} %bitcast.10, s32[1,16]{1,0:T(1,128)S(1)} %copy-done.3, bf16[16,256,128]{2,1,0:T(8,128)(2,1)S(1)} %get-tuple-element.7.pieces_ref, bf16[16,8,128,128]{3,2,1,0:T(8,128)(2,1)S(1)} %get-tuple-element.8.values_ref), custom_call_target="tpu_custom_call" | custom-call | tf_op jit(solution)/shard_map/tile_products/pallas_call | solution.py:306
  34.6 23.6 %scatter_sums.1 = f32[256,128]{1,0:T(8,128)S(1)} custom-call(bf16[2,8,2,2,128,128]{5,4,3,2,1,0:T(8,128)(2,1)S(1)} %tile_products.1.part_ref), custom_call_target="tpu_custom_call" | custom-call | bytes 50331648 | tf_op jit(solution)/shard_map/scatter_sums/pallas_call | solution.py:321
  58.2 0.0 copy-done
  58.2 0.0 copy-done.4
  58.2 0.0 copy-done.5
  58.2 0.9 %fusion.1 = bf16[256,128]{1,0:T(8,128)(2,1)} fusion(bf16[128,128]{1,0:T(8,128)(2,1)S(1)} %copy-done, f32[256,128]{1,0:T(8,128)S(1)} %scatter_sums.1, f32[128]{0:T(128)S(1)} %copy-done.5, f32[256]{0:T(256)S(1)} %copy-done.4), kind=kOutput, calls=%fused_computation.2 | convolution fusion | flops 8552448 | bytes 230912 | tf_op jit(solution)/shard_map/dot_general | solution.py:350
Async XLA Ops:
  0.0 58.2 %copy-start = (bf16[128,128]{1,0:T(8,128)(2,1)S(1)}, bf16[128,128]{1,0:T(8,128)(2,1)}, u32[]{:S(2)}) copy-start(bf16[128,128]{1,0:T(8,128)(2,1)} %param.10) | copy-start | bytes 98308
  0.0 28.6 %copy-start.3 = (s32[1,16]{1,0:T(1,128)S(1)}, s32[1,16]{1,0:T(1,128)}, u32[]{:S(2)}) copy-start(s32[1,16]{1,0:T(1,128)} %counts_hbm.1) | copy-start | bytes 196
  0.0 28.6 %copy-start.2 = (s32[1,16,8]{1,2,0:T(8,128)S(1)}, s32[1,16,8]{1,2,0:T(8,128)}, u32[]{:S(2)}) copy-start(s32[1,16,8]{1,2,0:T(8,128)} %param.14) | copy-start | bytes 1540
  0.0 28.6 %copy-start.1 = (s32[1,16,8]{1,2,0:T(8,128)S(1)}, s32[1,16,8]{1,2,0:T(8,128)}, u32[]{:S(2)}) copy-start(s32[1,16,8]{1,2,0:T(8,128)} %param.13) | copy-start | bytes 1540
  28.6 29.6 %copy-start.4 = (f32[256]{0:T(256)S(1)}, f32[256]{0:T(256)}, u32[]{:S(2)}) copy-start(f32[256]{0:T(256)} %param.9) | copy-start | bytes 3076
  28.7 29.6 %copy-start.5 = (f32[128]{0:T(128)S(1)}, f32[128]{0:T(128)}, u32[]{:S(2)}) copy-start(f32[128]{0:T(128)} %param.11) | copy-start | bytes 1540

commit v4 on v2

--- a/solution.py
+++ b/solution.py
@@ -17,8 +17,8 @@
 
 
 def gather_kernel(
-    features_hbm, inv_hbm, values_hbm, out_ref, values_ref,
-    features_ref, inv_ref, send_sems, recv_sems, load_sems, value_sems,
+    features_hbm, inv_hbm, values_hbm, products_ref,
+    out_ref, values_ref, features_ref, inv_ref, send_sems, recv_sems, load_sems, value_sems,
 ):
     me = lax.axis_index("section")
     x, z = me // 4, me % 4
@@ -80,9 +80,23 @@
             device_id_type=MESH,
         ).wait_recv()
 
+    def product(dx, dz):
+        if (dx, dz) != (0, 0):
+            need(dx, dz, 0)
+            need(dx, dz, 1)
+        slot = sec(dx, dz)
+        caps, tile = values_ref.shape[1:3]
+        right = jnp.concatenate([out_ref[slot, 0:tile, :], out_ref[slot, tile:, :]], axis=1)
+        left = values_ref[slot].reshape(caps * tile, tile)
+        both = jnp.dot(left, right, preferred_element_type=jnp.float32)
+        for c in range(2):
+            products_ref[slot, c] = both[:, c * tile : (c + 1) * tile].reshape(caps, tile, tile)
+
     for h, peer in ((0, zp), (1, zm), (1, zp), (0, zm), (0, xp), (1, xm), (1, xp), (0, xm)):
         send(me, h, peer)
-
+    for fill in fills:
+        fill.wait()
+    product(0, 0)
     need(0, 3, 0)
     send(sec(0, 3), 0, zp)
     need(0, 1, 1)
@@ -101,6 +115,10 @@
     need(0, 1, 0)
     send(sec(0, 1), 0, xp)
     send(sec(0, 1), 0, xm)
+    product(3, 0)
+    product(1, 0)
+    product(0, 3)
+    product(0, 1)
     need(3, 3, 0)
     send(sec(3, 3), 0, xp)
     need(1, 1, 1)
@@ -111,27 +129,26 @@
     need(0, 2, 1)
     send(sec(0, 2), 1, xm)
     send(sec(0, 2), 1, xp)
+    product(0, 2)
     need(1, 3, 1)
     send(sec(1, 3), 1, xm)
     need(3, 1, 0)
     send(sec(3, 1), 0, xp)
+    product(2, 0)
+    product(3, 3)
+    product(1, 1)
     need(3, 2, 0)
     send(sec(3, 2), 0, xp)
     need(1, 2, 1)
     send(sec(1, 2), 1, xm)
-    for dx in range(4):
-        for dz in range(4):
-            for h in range(2):
-                if (dx, dz) != (0, 0):
-                    need(dx, dz, h)
-    for fill in fills:
-        fill.wait()
+    for dx, dz in ((1, 3), (3, 1), (2, 3), (2, 1), (3, 2), (1, 2), (2, 2)):
+        product(dx, dz)
     for copy in sends:
         copy.wait_send()
 
 
 def tiles_kernel(
-    rows_hbm, cols_hbm, counts_hbm, pieces_ref, values_ref, out_ref,
+    rows_hbm, cols_hbm, counts_hbm, products_ref, out_ref,
     rows_ref, cols_ref, counts_ref, total, sems,
 ):
     loads = [
@@ -143,20 +160,17 @@
     for load in loads:
         load.start()
     caps, sections = rows_ref.shape
-    tile = total.shape[1]
     tile_rows = total.shape[0] - 1
     total[...] = jnp.zeros_like(total)
     for load in loads:
         load.wait()
 
     def body(t, carry):
-        right = jnp.concatenate([pieces_ref[t, 0:tile, :], pieces_ref[t, tile : 2 * tile, :]], axis=1)
-        left = values_ref[t].reshape(caps * tile, tile)
-        both = jnp.dot(left, right, preferred_element_type=jnp.float32)
         for k in range(caps):
-            row = jnp.where(k < counts_ref[0, t], rows_ref[k, t], tile_rows)
-            part = both[k * tile : (k + 1) * tile, :]
-            total[row] += jnp.where(cols_ref[k, t] == 0, part[:, :tile], part[:, tile:])
+            live = k < counts_ref[0, t]
+            row = jnp.where(live, rows_ref[k, t], tile_rows)
+            col = jnp.where(live, cols_ref[k, t], 0)
+            total[row] += products_ref[t, col, k]
         return carry
 
     lax.fori_loop(0, sections, body, 0)
@@ -276,15 +290,14 @@
     hbm = pl.BlockSpec(memory_space=pltpu.HBM)
     bf16, f32 = jnp.bfloat16, jnp.float32
     dma = pltpu.SemaphoreType.DMA
-    pieces, values = pl.pallas_call(
+    products = pl.pallas_call(
         gather_kernel,
-        out_shape=(
-            pltpu.VMEM((16, rows_dev, width), bf16),
+        out_shape=pltpu.VMEM((sections, 2, caps, tile, width), f32),
+        in_specs=[hbm, hbm, hbm],
+        out_specs=vmem,
+        scratch_shapes=[
+            pltpu.VMEM((sections, rows_dev, width), bf16),
             pltpu.VMEM(tile_values.shape[1:], bf16),
-        ),
-        in_specs=[hbm, hbm, hbm],
-        out_specs=(vmem, vmem),
-        scratch_shapes=[
             pltpu.VMEM((rows_dev, width), bf16),
             pltpu.VMEM((2, rows_dev // 2), f32),
             dma((30,)),
@@ -293,7 +306,7 @@
             dma((sections,)),
         ],
         compiler_params=pltpu.CompilerParams(
-            collective_id=0, has_side_effects=True, vmem_limit_bytes=57 * MIB
+            collective_id=0, has_side_effects=True, vmem_limit_bytes=46 * MIB
         ),
         cost_estimate=pl.CostEstimate(flops=0, bytes_accessed=48 * MIB, transcendentals=0),
         name="gather_pieces",
@@ -301,7 +314,7 @@
     partial = pl.pallas_call(
         tiles_kernel,
         out_shape=jax.ShapeDtypeStruct((2, 8, 2, 2, tile, width), bf16),
-        in_specs=[hbm, hbm, hbm, vmem, vmem],
+        in_specs=[hbm, hbm, hbm, vmem],
         out_specs=vmem,
         scratch_shapes=[
             pltpu.SMEM((caps, sections), jnp.int32),
@@ -312,7 +325,7 @@
         ],
         compiler_params=pltpu.CompilerParams(vmem_limit_bytes=20 * MIB),
         name="tile_products",
-    )(tile_rows[0].T, tile_cols[0].T, tile_counts, pieces, values)
+    )(tile_rows[0].T, tile_cols[0].T, tile_counts, products)
     summed = pl.pallas_call(
         scatter_kernel,
         out_shape=jax.ShapeDtypeStruct((rows_dev, width), f32),

time: 56.1 us -> 52.7 us (0.939)
  Pallas kernels: 54.9 us -> 51.4 us
    pallas_call x1, Pallas kernels: 5.83 us -> 2.02 us  [shards(): pl.pallas_call(tiles_kernel, out_shape=jax.ShapeDtypeStruct((2, 8, 2, 2,...]
where the time goes in v4:
time: 52.7 us; the launch traced here: 52.4 us
  Pallas kernels  51.4 us (98%)
  matrix products  0.86 us (2%)
    pallas_call x1, Pallas kernels, shards(): pl.pallas_call(gather_kernel, out_shape=pltpu.VMEM((sections, 2, caps, ti...  25.1 us
    pallas_call x1, Pallas kernels, shards(): pl.pallas_call(scatter_kernel, out_shape=jax.ShapeDtypeStruct((rows_dev,...  24.2 us
    pallas_call x1, Pallas kernels, shards(): pl.pallas_call(tiles_kernel, out_shape=jax.ShapeDtypeStruct((2, 8, 2, 2,...  2.02 us

profile of v4, /device:TPU:6, one launch (start us, length us, event | category | flops | bytes accessed | tf_op | source)
XLA Modules:
  0.0 52.4 jit_solution(11937873690469287492)
XLA Ops:
  0.0 0.0 copy-start
  0.0 0.0 copy-start.1
  0.0 0.0 copy-start.2
  0.0 0.0 copy-start.3
  0.0 25.1 %gather_pieces.1.products_ref = f32[16,2,8,128,128]{4,3,2,1,0:T(8,128)S(1)} custom-call(bf16[256,128]{1,0:T(8,128)(2,1)} %features_hbm.1, f32[2,128]{1,0:T(2,128)} %bitcast.12, bf16[16,8,128,128]{3,2,1,0:T(8,128)(2,1)} %bitcast.11), custom_call_target="tpu_custom_call" | custom-call | bytes 50331648 | tf_op jit(solution)/shard_map/gather_pieces/pallas_call | solution.py:293
  25.2 0.0 copy-done.1
  25.2 0.0 copy-done.2
  25.2 0.0 copy-done.3
  25.2 0.0 copy-start.4
  25.2 0.0 copy-start.5
  25.2 2.0 %tile_products.1.part_ref = bf16[2,8,2,2,128,128]{5,4,3,2,1,0:T(8,128)(2,1)S(1)} custom-call(s32[8,16]{1,0:T(8,128)S(1)} %bitcast.9, s32[8,16]{1,0:T(8,128)S(1)} %bitcast.10, s32[1,16]{1,0:T(1,128)S(1)} %copy-done.3, f32[16,2,8,128,128]{4,3,2,1,0:T(8,128)S(1)} %gather_pieces.1.products_ref), custom_call_target="tpu_custom_call" | custom-call | tf_op jit(solution)/shard_map/tile_products/pallas_call | solution.py:314
  27.3 24.2 %scatter_sums.1 = f32[256,128]{1,0:T(8,128)S(1)} custom-call(bf16[2,8,2,2,128,128]{5,4,3,2,1,0:T(8,128)(2,1)S(1)} %tile_products.1.part_ref), custom_call_target="tpu_custom_call" | custom-call | bytes 50331648 | tf_op jit(solution)/shard_map/scatter_sums/pallas_call | solution.py:329
  51.5 0.0 copy-done
  51.5 0.0 copy-done.4
  51.5 0.0 copy-done.5
  51.5 0.9 %fusion.1 = bf16[256,128]{1,0:T(8,128)(2,1)} fusion(bf16[128,128]{1,0:T(8,128)(2,1)S(1)} %copy-done, f32[256,128]{1,0:T(8,128)S(1)} %scatter_sums.1, f32[128]{0:T(128)S(1)} %copy-done.5, f32[256]{0:T(256)S(1)} %copy-done.4), kind=kOutput, calls=%fused_computation.2 | convolution fusion | flops 8552448 | bytes 230912 | tf_op jit(solution)/shard_map/dot_general | solution.py:354
Async XLA Ops:
  0.0 51.5 %copy-start = (bf16[128,128]{1,0:T(8,128)(2,1)S(1)}, bf16[128,128]{1,0:T(8,128)(2,1)}, u32[]{:S(2)}) copy-start(bf16[128,128]{1,0:T(8,128)(2,1)} %param.10) | copy-start | bytes 98308
  0.0 25.2 %copy-start.1 = (s32[1,16,8]{1,2,0:T(8,128)S(1)}, s32[1,16,8]{1,2,0:T(8,128)}, u32[]{:S(2)}) copy-start(s32[1,16,8]{1,2,0:T(8,128)} %param.13) | copy-start | bytes 1540
  0.0 25.2 %copy-start.2 = (s32[1,16,8]{1,2,0:T(8,128)S(1)}, s32[1,16,8]{1,2,0:T(8,128)}, u32[]{:S(2)}) copy-start(s32[1,16,8]{1,2,0:T(8,128)} %param.14) | copy-start | bytes 1540
  0.0 25.2 %copy-start.3 = (s32[1,16]{1,0:T(1,128)S(1)}, s32[1,16]{1,0:T(1,128)}, u32[]{:S(2)}) copy-start(s32[1,16]{1,0:T(1,128)} %counts_hbm.1) | copy-start | bytes 196
  25.2 26.3 %copy-start.4 = (f32[256]{0:T(256)S(1)}, f32[256]{0:T(256)}, u32[]{:S(2)}) copy-start(f32[256]{0:T(256)} %param.9) | copy-start | bytes 3076
  25.2 26.3 %copy-start.5 = (f32[128]{0:T(128)S(1)}, f32[128]{0:T(128)}, u32[]{:S(2)}) copy-start(f32[128]{0:T(128)} %param.11) | copy-start | bytes 1540

commit v5 on v4

--- a/solution.py
+++ b/solution.py
@@ -52,7 +52,7 @@
     sends = []
 
     def send(slot, h, peer):
-        rows = pl.ds(h * half, half)
+        rows = pl.ds(h * (half // 2), half // 2)
         copy = pltpu.make_async_remote_copy(
             src_ref=out_ref.at[slot, rows],
             dst_ref=out_ref.at[slot, rows],
@@ -70,7 +70,7 @@
         if (dx, dz, h) in waited:
             return
         waited.add((dx, dz, h))
-        slot, rows = sec(dx, dz), pl.ds(h * half, half)
+        slot, rows = sec(dx, dz), pl.ds(h * (half // 2), half // 2)
         pltpu.make_async_remote_copy(
             src_ref=out_ref.at[slot, rows],
             dst_ref=out_ref.at[slot, rows],
@@ -82,8 +82,8 @@
 
     def product(dx, dz):
         if (dx, dz) != (0, 0):
-            need(dx, dz, 0)
-            need(dx, dz, 1)
+            for q in range(4):
+                need(dx, dz, q)
         slot = sec(dx, dz)
         caps, tile = values_ref.shape[1:3]
         right = jnp.concatenate([out_ref[slot, 0:tile, :], out_ref[slot, tile:, :]], axis=1)
@@ -92,55 +92,37 @@
         for c in range(2):
             products_ref[slot, c] = both[:, c * tile : (c + 1) * tile].reshape(caps, tile, tile)
 
-    for h, peer in ((0, zp), (1, zm), (1, zp), (0, zm), (0, xp), (1, xm), (1, xp), (0, xm)):
-        send(me, h, peer)
+    def relay(*items):
+        for g in range(2):
+            for dx, dz, h, peers in items:
+                if (dx, dz) != (0, 0):
+                    need(dx, dz, 2 * h + g)
+                for peer in peers:
+                    send(sec(dx, dz), 2 * h + g, peer)
+
+    relay((0, 0, 0, (zp,)), (0, 0, 1, (zm,)))
+    relay((0, 0, 1, (zp,)), (0, 0, 0, (zm,)))
+    relay((0, 0, 0, (xp,)), (0, 0, 1, (xm,)))
+    relay((0, 0, 1, (xp,)), (0, 0, 0, (xm,)))
     for fill in fills:
         fill.wait()
     product(0, 0)
-    need(0, 3, 0)
-    send(sec(0, 3), 0, zp)
-    need(0, 1, 1)
-    send(sec(0, 1), 1, zm)
-    send(sec(0, 3), 0, xp)
-    send(sec(0, 1), 1, xm)
-    need(3, 0, 0)
-    send(sec(3, 0), 0, xp)
-    need(1, 0, 1)
-    send(sec(1, 0), 1, xm)
-    send(sec(0, 1), 1, xp)
-    send(sec(0, 3), 0, xm)
-    need(0, 3, 1)
-    send(sec(0, 3), 1, xp)
-    send(sec(0, 3), 1, xm)
-    need(0, 1, 0)
-    send(sec(0, 1), 0, xp)
-    send(sec(0, 1), 0, xm)
+    relay((0, 3, 0, (zp, xp)), (0, 1, 1, (zm, xm)))
+    relay((3, 0, 0, (xp,)), (1, 0, 1, (xm,)))
+    relay((0, 1, 1, (xp,)), (0, 3, 0, (xm,)))
+    relay((0, 3, 1, (xp, xm)), (0, 1, 0, (xp, xm)))
     product(3, 0)
     product(1, 0)
     product(0, 3)
     product(0, 1)
-    need(3, 3, 0)
-    send(sec(3, 3), 0, xp)
-    need(1, 1, 1)
-    send(sec(1, 1), 1, xm)
-    need(0, 2, 0)
-    send(sec(0, 2), 0, xp)
-    send(sec(0, 2), 0, xm)
-    need(0, 2, 1)
-    send(sec(0, 2), 1, xm)
-    send(sec(0, 2), 1, xp)
+    relay((3, 3, 0, (xp,)), (1, 1, 1, (xm,)))
+    relay((0, 2, 0, (xp, xm)), (0, 2, 1, (xm, xp)))
     product(0, 2)
-    need(1, 3, 1)
-    send(sec(1, 3), 1, xm)
-    need(3, 1, 0)
-    send(sec(3, 1), 0, xp)
+    relay((1, 3, 1, (xm,)), (3, 1, 0, (xp,)))
     product(2, 0)
     product(3, 3)
     product(1, 1)
-    need(3, 2, 0)
-    send(sec(3, 2), 0, xp)
-    need(1, 2, 1)
-    send(sec(1, 2), 1, xm)
+    relay((3, 2, 0, (xp,)), (1, 2, 1, (xm,)))
     for dx, dz in ((1, 3), (3, 1), (2, 3), (2, 1), (3, 2), (1, 2), (2, 2)):
         product(dx, dz)
     for copy in sends:
@@ -177,10 +159,11 @@
     for core in range(2):
         for y in range(8):
             for z in range(2):
-                for h in range(2):
-                    out_ref[core, y, z, h] = total[((z * 8 + y) * 2 + core) * 2 + h].astype(
-                        out_ref.dtype
-                    )
+                for h in range(4):
+                    rows = slice(h % 2 * 64, h % 2 * 64 + 64)
+                    out_ref[core, y, z, h] = total[
+                        ((z * 8 + y) * 2 + core) * 2 + h // 2, rows, :
+                    ].astype(out_ref.dtype)
 
 
 def scatter_kernel(
@@ -189,7 +172,7 @@
 ):
     me = lax.axis_index("rep")
     core, y, z = me % 2, (me // 2) % 8, me // 16
-    tile = out_ref.shape[0] // 2
+    part = out_ref.shape[0] // 4
 
     def rep(zz, yy, cc):
         return (zz * 8 + yy % 8) * 2 + cc
@@ -223,12 +206,12 @@
         return part_ref[core, at, zz, h].astype(jnp.float32) + mate[at, zz, h].astype(jnp.float32)
 
     def hops(d, h):
-        return 4 if d != h else 3
+        return 4 if d != h // 2 else 3
 
     copies = {}
     for s in range(4):
         for zi in range(2):
-            for d, h in ((0, 1), (1, 0), (0, 0), (1, 1)):
+            for d, h in ((0, 2), (1, 0), (0, 3), (1, 1), (0, 0), (1, 2), (0, 1), (1, 3)):
                 length = hops(d, h)
                 if s >= length:
                     continue
@@ -260,7 +243,7 @@
         return value
 
     crosses = []
-    for h in range(2):
+    for h in range(4):
         zout[h] = gathered(0, h).astype(jnp.bfloat16)
         crosses.append(
             pltpu.make_async_remote_copy(
@@ -273,10 +256,10 @@
             )
         )
         crosses[h].start()
-    mine = [gathered(1, h) for h in range(2)]
-    for h in range(2):
+    mine = [gathered(1, h) for h in range(4)]
+    for h in range(4):
         crosses[h].wait_recv()
-        out_ref[h * tile : (h + 1) * tile, :] = mine[h] + zin[h].astype(jnp.float32)
+        out_ref[h * part : (h + 1) * part, :] = mine[h] + zin[h].astype(jnp.float32)
     for copy in list(swaps.values()) + list(copies.values()) + crosses:
         copy.wait_send()
 
@@ -300,8 +283,8 @@
             pltpu.VMEM(tile_values.shape[1:], bf16),
             pltpu.VMEM((rows_dev, width), bf16),
             pltpu.VMEM((2, rows_dev // 2), f32),
-            dma((30,)),
-            dma((16, 2)),
+            dma((60,)),
+            dma((16, 4)),
             dma((2,)),
             dma((sections,)),
         ],
@@ -313,7 +296,7 @@
     )(features, inv_degree.reshape(2, rows_dev // 2), tile_values[0])
     partial = pl.pallas_call(
         tiles_kernel,
-        out_shape=jax.ShapeDtypeStruct((2, 8, 2, 2, tile, width), bf16),
+        out_shape=jax.ShapeDtypeStruct((2, 8, 2, 4, tile // 2, width), bf16),
         in_specs=[hbm, hbm, hbm, vmem],
         out_specs=vmem,
         scratch_shapes=[
@@ -332,17 +315,17 @@
         in_specs=[vmem],
         out_specs=vmem,
         scratch_shapes=[
-            pltpu.VMEM((8, 2, 2, tile, width), bf16),
-            pltpu.VMEM((2, 2, 2, tile, width), bf16),
-            pltpu.VMEM((2, 2, 2, 4, tile, width), bf16),
-            pltpu.VMEM((2, tile, width), bf16),
-            pltpu.VMEM((2, tile, width), bf16),
+            pltpu.VMEM((8, 2, 4, tile // 2, width), bf16),
+            pltpu.VMEM((2, 4, 2, tile // 2, width), bf16),
+            pltpu.VMEM((2, 4, 2, 4, tile // 2, width), bf16),
+            pltpu.VMEM((4, tile // 2, width), bf16),
+            pltpu.VMEM((4, tile // 2, width), bf16),
             dma((8,)),
             dma((8,)),
-            dma((2, 2, 2, 4)),
-            dma((2, 2, 2, 4)),
-            dma((2,)),
-            dma((2,)),
+            dma((2, 4, 2, 4)),
+            dma((2, 4, 2, 4)),
+            dma((4,)),
+            dma((4,)),
         ],
         compiler_params=pltpu.CompilerParams(
             collective_id=1, has_side_effects=True, vmem_limit_bytes=16 * MIB

time: 52.7 us -> 53.1 us (level)
    pallas_call x1, Pallas kernels: 24.2 us -> 22.9 us  [shards(): pl.pallas_call(scatter_kernel, out_shape=jax.ShapeDtypeStruct((rows_dev,...]
    pallas_call x1, Pallas kernels: 25.1 us -> 26.4 us  [shards(): pl.pallas_call(gather_kernel, out_shape=pltpu.VMEM((sections, 2, caps, ti...]
where the time goes in v5:
time: 53.1 us; the launch traced here: 52.3 us
  Pallas kernels  51.3 us (97%)
  matrix products  0.86 us (2%)
    pallas_call x1, Pallas kernels, shards(): pl.pallas_call(gather_kernel, out_shape=pltpu.VMEM((sections, 2, caps, ti...  26.4 us
    pallas_call x1, Pallas kernels, shards(): pl.pallas_call(scatter_kernel, out_shape=jax.ShapeDtypeStruct((rows_dev,...  22.9 us
    pallas_call x1, Pallas kernels, shards(): pl.pallas_call(tiles_kernel, out_shape=jax.ShapeDtypeStruct((2, 8, 2, 4,...  2.05 us

profile of v5, /device:TPU:6, one launch (start us, length us, event | category | flops | bytes accessed | tf_op | source)
XLA Modules:
  0.0 52.3 jit_solution(17496205752449658732)
XLA Ops:
  0.0 0.0 copy-start
  0.0 0.0 copy-start.1
  0.0 0.0 copy-start.2
  0.0 0.0 copy-start.3
  0.0 26.4 %gather_pieces.1.products_ref = f32[16,2,8,128,128]{4,3,2,1,0:T(8,128)S(1)} custom-call(bf16[256,128]{1,0:T(8,128)(2,1)} %features_hbm.1, f32[2,128]{1,0:T(2,128)} %bitcast.12, bf16[16,8,128,128]{3,2,1,0:T(8,128)(2,1)} %bitcast.11), custom_call_target="tpu_custom_call" | custom-call | bytes 50331648 | tf_op jit(solution)/shard_map/gather_pieces/pallas_call | solution.py:276
  26.4 0.0 copy-done.1
  26.4 0.0 copy-done.2
  26.4 0.0 copy-done.3
  26.4 0.0 copy-start.4
  26.4 0.0 copy-start.5
  26.4 2.0 %tile_products.1.part_ref = bf16[2,8,2,4,64,128]{5,4,3,2,1,0:T(8,128)(2,1)S(1)} custom-call(s32[8,16]{1,0:T(8,128)S(1)} %bitcast.9, s32[8,16]{1,0:T(8,128)S(1)} %bitcast.10, s32[1,16]{1,0:T(1,128)S(1)} %copy-done.3, f32[16,2,8,128,128]{4,3,2,1,0:T(8,128)S(1)} %gather_pieces.1.products_ref), custom_call_target="tpu_custom_call" | custom-call | tf_op jit(solution)/shard_map/tile_products/pallas_call | solution.py:297
  28.5 22.9 %scatter_sums.1 = f32[256,128]{1,0:T(8,128)S(1)} custom-call(bf16[2,8,2,4,64,128]{5,4,3,2,1,0:T(8,128)(2,1)S(1)} %tile_products.1.part_ref), custom_call_target="tpu_custom_call" | custom-call | bytes 50331648 | tf_op jit(solution)/shard_map/scatter_sums/pallas_call | solution.py:312
  51.4 0.0 copy-done
  51.4 0.0 copy-done.4
  51.5 0.0 copy-done.5
  51.5 0.9 %fusion.1 = bf16[256,128]{1,0:T(8,128)(2,1)} fusion(bf16[128,128]{1,0:T(8,128)(2,1)S(1)} %copy-done, f32[256,128]{1,0:T(8,128)S(1)} %scatter_sums.1, f32[128]{0:T(128)S(1)} %copy-done.5, f32[256]{0:T(256)S(1)} %copy-done.4), kind=kOutput, calls=%fused_computation.2 | convolution fusion | flops 8552448 | bytes 230912 | tf_op jit(solution)/shard_map/dot_general | solution.py:337
Async XLA Ops:
  0.0 51.4 %copy-start = (bf16[128,128]{1,0:T(8,128)(2,1)S(1)}, bf16[128,128]{1,0:T(8,128)(2,1)}, u32[]{:S(2)}) copy-start(bf16[128,128]{1,0:T(8,128)(2,1)} %param.10) | copy-start | bytes 98308
  0.0 26.4 %copy-start.1 = (s32[1,16,8]{1,2,0:T(8,128)S(1)}, s32[1,16,8]{1,2,0:T(8,128)}, u32[]{:S(2)}) copy-start(s32[1,16,8]{1,2,0:T(8,128)} %param.13) | copy-start | bytes 1540
  0.0 26.4 %copy-start.2 = (s32[1,16,8]{1,2,0:T(8,128)S(1)}, s32[1,16,8]{1,2,0:T(8,128)}, u32[]{:S(2)}) copy-start(s32[1,16,8]{1,2,0:T(8,128)} %param.14) | copy-start | bytes 1540
  0.0 26.4 %copy-start.3 = (s32[1,16]{1,0:T(1,128)S(1)}, s32[1,16]{1,0:T(1,128)}, u32[]{:S(2)}) copy-start(s32[1,16]{1,0:T(1,128)} %counts_hbm.1) | copy-start | bytes 196
  26.4 25.0 %copy-start.4 = (f32[256]{0:T(256)S(1)}, f32[256]{0:T(256)}, u32[]{:S(2)}) copy-start(f32[256]{0:T(256)} %param.9) | copy-start | bytes 3076
  26.4 25.0 %copy-start.5 = (f32[128]{0:T(128)S(1)}, f32[128]{0:T(128)}, u32[]{:S(2)}) copy-start(f32[128]{0:T(128)} %param.11) | copy-start | bytes 1540

commit v6 on v5

--- a/solution.py
+++ b/solution.py
@@ -203,7 +203,25 @@
             swaps[dy].wait_recv()
         at = (y + dy) % 8
         zz = 1 - z if zi == 0 else z
-        return part_ref[core, at, zz, h].astype(jnp.float32) + mate[at, zz, h].astype(jnp.float32)
+        value = part_ref[core, at, zz, h].astype(jnp.float32) + mate[at, zz, h].astype(jnp.float32)
+        if (zi, h) == (1, 3):
+            crosses[dy].wait_recv()
+            value = value + zin[dy].astype(jnp.float32)
+        return value
+
+    crosses = {}
+
+    def cross(n, value):
+        zout[n] = value.astype(jnp.bfloat16)
+        crosses[n] = pltpu.make_async_remote_copy(
+            src_ref=zout.at[n],
+            dst_ref=zin.at[n],
+            send_sem=z_send.at[n],
+            recv_sem=z_recv.at[n],
+            device_id={"rep": across},
+            device_id_type=MESH,
+        )
+        crosses[n].start()
 
     def hops(d, h):
         return 4 if d != h // 2 else 3
@@ -211,9 +229,12 @@
     copies = {}
     for s in range(4):
         for zi in range(2):
-            for d, h in ((0, 2), (1, 0), (0, 3), (1, 1), (0, 0), (1, 2), (0, 1), (1, 3)):
+            if (s, zi) == (0, 1):
+                for dy in (4, 5, 3, 6, 2, 7, 1, 0):
+                    cross(dy, term(dy, 0, 3))
+            for d, h in ((0, 2), (1, 0), (1, 1), (0, 0), (1, 2), (0, 1), (0, 3), (1, 3)):
                 length = hops(d, h)
-                if s >= length:
+                if s >= length or (zi, h) == (0, 3):
                     continue
                 dy = (length - s) * (1 - 2 * d)
                 value = term(dy, zi, h)
@@ -242,25 +263,14 @@
             value = value + runs[d, h, zi, last].astype(jnp.float32)
         return value
 
-    crosses = []
-    for h in range(4):
-        zout[h] = gathered(0, h).astype(jnp.bfloat16)
-        crosses.append(
-            pltpu.make_async_remote_copy(
-                src_ref=zout.at[h],
-                dst_ref=zin.at[h],
-                send_sem=z_send.at[h],
-                recv_sem=z_recv.at[h],
-                device_id={"rep": across},
-                device_id_type=MESH,
-            )
-        )
-        crosses[h].start()
+    for h in range(3):
+        cross(8 + h, gathered(0, h))
     mine = [gathered(1, h) for h in range(4)]
-    for h in range(4):
-        crosses[h].wait_recv()
-        out_ref[h * part : (h + 1) * part, :] = mine[h] + zin[h].astype(jnp.float32)
-    for copy in list(swaps.values()) + list(copies.values()) + crosses:
+    out_ref[3 * part :, :] = mine[3]
+    for h in range(3):
+        crosses[8 + h].wait_recv()
+        out_ref[h * part : (h + 1) * part, :] = mine[h] + zin[8 + h].astype(jnp.float32)
+    for copy in list(swaps.values()) + list(copies.values()) + list(crosses.values()):
         copy.wait_send()
 
 
@@ -318,14 +328,14 @@
             pltpu.VMEM((8, 2, 4, tile // 2, width), bf16),
             pltpu.VMEM((2, 4, 2, tile // 2, width), bf16),
             pltpu.VMEM((2, 4, 2, 4, tile // 2, width), bf16),
-            pltpu.VMEM((4, tile // 2, width), bf16),
-            pltpu.VMEM((4, tile // 2, width), bf16),
+            pltpu.VMEM((11, tile // 2, width), bf16),
+            pltpu.VMEM((11, tile // 2, width), bf16),
             dma((8,)),
             dma((8,)),
             dma((2, 4, 2, 4)),
             dma((2, 4, 2, 4)),
-            dma((4,)),
-            dma((4,)),
+            dma((11,)),
+            dma((11,)),
         ],
         compiler_params=pltpu.CompilerParams(
             collective_id=1, has_side_effects=True, vmem_limit_bytes=16 * MIB

time: 53.1 us -> 53.2 us (level)
  no operation moved by 1% of the time
where the time goes in v6:
time: 53.2 us; the launch traced here: 52.1 us
  Pallas kernels  51.2 us (96%)
  matrix products  0.86 us (2%)
    pallas_call x1, Pallas kernels, shards(): pl.pallas_call(gather_kernel, out_shape=pltpu.VMEM((sections, 2, caps, ti...  26.4 us
    pallas_call x1, Pallas kernels, shards(): pl.pallas_call(scatter_kernel, out_shape=jax.ShapeDtypeStruct((rows_dev,...  22.7 us
    pallas_call x1, Pallas kernels, shards(): pl.pallas_call(tiles_kernel, out_shape=jax.ShapeDtypeStruct((2, 8, 2, 4,...  2.08 us

profile of v6, /device:TPU:6, one launch (start us, length us, event | category | flops | bytes accessed | tf_op | source)
XLA Modules:
  0.0 52.1 jit_solution(16325074001372266762)
XLA Ops:
  0.0 0.0 copy-start
  0.0 0.0 copy-start.1
  0.0 0.0 copy-start.2
  0.0 0.0 copy-start.3
  0.0 26.4 %gather_pieces.1.products_ref = f32[16,2,8,128,128]{4,3,2,1,0:T(8,128)S(1)} custom-call(bf16[256,128]{1,0:T(8,128)(2,1)} %features_hbm.1, f32[2,128]{1,0:T(2,128)} %bitcast.12, bf16[16,8,128,128]{3,2,1,0:T(8,128)(2,1)} %bitcast.11), custom_call_target="tpu_custom_call" | custom-call | bytes 50331648 | tf_op jit(solution)/shard_map/gather_pieces/pallas_call | solution.py:286
  26.4 0.0 copy-done.1
  26.4 0.0 copy-done.2
  26.4 0.0 copy-done.3
  26.4 0.0 copy-start.4
  26.4 0.0 copy-start.5
  26.4 2.1 %tile_products.1.part_ref = bf16[2,8,2,4,64,128]{5,4,3,2,1,0:T(8,128)(2,1)S(1)} custom-call(s32[8,16]{1,0:T(8,128)S(1)} %bitcast.9, s32[8,16]{1,0:T(8,128)S(1)} %bitcast.10, s32[1,16]{1,0:T(1,128)S(1)} %copy-done.3, f32[16,2,8,128,128]{4,3,2,1,0:T(8,128)S(1)} %gather_pieces.1.products_ref), custom_call_target="tpu_custom_call" | custom-call | tf_op jit(solution)/shard_map/tile_products/pallas_call | solution.py:307
  28.5 22.7 %scatter_sums.1 = f32[256,128]{1,0:T(8,128)S(1)} custom-call(bf16[2,8,2,4,64,128]{5,4,3,2,1,0:T(8,128)(2,1)S(1)} %tile_products.1.part_ref), custom_call_target="tpu_custom_call" | custom-call | bytes 50331648 | tf_op jit(solution)/shard_map/scatter_sums/pallas_call | solution.py:322
  51.3 0.0 copy-done
  51.3 0.0 copy-done.4
  51.3 0.0 copy-done.5
  51.3 0.9 %fusion.1 = bf16[256,128]{1,0:T(8,128)(2,1)} fusion(bf16[128,128]{1,0:T(8,128)(2,1)S(1)} %copy-done, f32[256,128]{1,0:T(8,128)S(1)} %scatter_sums.1, f32[128]{0:T(128)S(1)} %copy-done.5, f32[256]{0:T(256)S(1)} %copy-done.4), kind=kOutput, calls=%fused_computation.2 | convolution fusion | flops 8552448 | bytes 230912 | tf_op jit(solution)/shard_map/dot_general | solution.py:347
Async XLA Ops:
  0.0 51.3 %copy-start = (bf16[128,128]{1,0:T(8,128)(2,1)S(1)}, bf16[128,128]{1,0:T(8,128)(2,1)}, u32[]{:S(2)}) copy-start(bf16[128,128]{1,0:T(8,128)(2,1)} %param.10) | copy-start | bytes 98308
  0.0 26.4 %copy-start.1 = (s32[1,16,8]{1,2,0:T(8,128)S(1)}, s32[1,16,8]{1,2,0:T(8,128)}, u32[]{:S(2)}) copy-start(s32[1,16,8]{1,2,0:T(8,128)} %param.13) | copy-start | bytes 1540
  0.0 26.4 %copy-start.2 = (s32[1,16,8]{1,2,0:T(8,128)S(1)}, s32[1,16,8]{1,2,0:T(8,128)}, u32[]{:S(2)}) copy-start(s32[1,16,8]{1,2,0:T(8,128)} %param.14) | copy-start | bytes 1540
  0.0 26.4 %copy-start.3 = (s32[1,16]{1,0:T(1,128)S(1)}, s32[1,16]{1,0:T(1,128)}, u32[]{:S(2)}) copy-start(s32[1,16]{1,0:T(1,128)} %counts_hbm.1) | copy-start | bytes 196
  26.4 24.9 %copy-start.4 = (f32[256]{0:T(256)S(1)}, f32[256]{0:T(256)}, u32[]{:S(2)}) copy-start(f32[256]{0:T(256)} %param.9) | copy-start | bytes 3076
  26.4 24.9 %copy-start.5 = (f32[128]{0:T(128)S(1)}, f32[128]{0:T(128)}, u32[]{:S(2)}) copy-start(f32[128]{0:T(128)} %param.11) | copy-start | bytes 1540
